TPU v7x, 32 devices: a whole 2x2x4 slice. The times are simulated.
32 devices in a mesh: box: 16 (over z, x, core), shift: 2 (over y).
Axes of the slice: x: 2, y: 2, z: 4, core: 2. Of those that a mesh axis runs over, the one named last changes fastest.
Arguments:
- vectors: bfloat16 [2, 1024, 128, 128], P('shift', 'box'), may hold values from -6 to 6
- sigma: float32 [2, 2], P('shift'), may hold values from 0.5 to 2
- near_blocks: bfloat16 [1024, 6, 128, 128], P('box', None, 'shift'), may hold values from -0.21875 to 0.21875
- near_index: int32 [1024, 6], P('box'), may hold values from -1 to 1023, as said below
- radiate: bfloat16 [128, 128], replicated, may hold values from -0.5 to 0.5
- interp_one: bfloat16 [8, 512, 128], replicated, may hold values from -0.1875 to 0.1875
- interp_two: bfloat16 [8, 2048, 512], replicated, may hold values from -0.09375 to 0.09375
- trans_one: float32 [316, 512], replicated, may hold values from -1.5 to 1.5
- level1_source: int32 [128, 16], P('box'), may hold values from -1 to 127, as said below
- level1_offset: int32 [128, 16], P('box'), may hold values from 0 to 315
- trans_two: float32 [316, 2048], P(None, 'box'), may hold values from -1 to 1
- level2_source: int32 [16, 32], replicated, may hold values from -1 to 15, as said below
- level2_offset: int32 [16, 32], replicated, may hold values from 0 to 315
Outputs:
- applied: float32 [2, 1024, 128, 128], P('shift', 'box')
Inputs may be any that keep to these rules, and one draw needn't show every extreme that they name: `near_index`: leaf boxes are numbered along a space-filling curve. Entry 0 of each row is the box itself; every live entry names a box within 64 of the row's box; live entries come first, unused ones are -1; some rows use all 6 entries and some only one. `level1_source`: entry 0 of each row is live; every live entry names a box within 8 of the row's box; live entries come first, unused ones are -1; some rows use all 16 entries and some only one. `level2_source`: entry 0 of each row is live; live entries come first, unused ones are -1; some rows use all 32 entries and some only one.
All inputs are finite; a program needn't handle non-finite values.
Results may differ from a plain program's by a relative error of at most 0.0035.
Values may be sent and summed in bfloat16 or wider, within the bound.
No kernel may reach another device: no remote copies, remote signals or barrier semaphores. Data moves between devices by JAX's collectives and lax.ppermute only.
A program may use at most 192 MiB of HBM per device.

v0:
```python
import functools

import jax
import jax.numpy as jnp
from jax import lax
from jax.experimental import pallas as pl
from jax.experimental.pallas import tpu as pltpu
from jax.sharding import PartitionSpec as P


F32 = jnp.float32
BF16 = jnp.bfloat16
NT = (((1,), (1,)), ((), ()))


def vmem():
    return pl.BlockSpec(memory_space=pltpu.VMEM)


def smem():
    return pl.BlockSpec(memory_space=pltpu.SMEM)


def cost(flops, moved):
    return pl.CostEstimate(flops=flops, bytes_accessed=moved, transcendentals=0)


def params(mib):
    return pltpu.CompilerParams(vmem_limit_bytes=mib << 20)


def fold_kernel(one_ref, radiate_ref, field_ref, fold_ref, upper_ref, turned_ref):
    children, _, _ = one_ref.shape
    unknowns = radiate_ref.shape[1]
    pair, _, columns = field_ref.shape

    @pl.when(pl.program_id(0) == 0)
    def _():
        for child in range(children):
            fold_ref[:, child * unknowns : (child + 1) * unknowns] = jnp.dot(
                one_ref[child], radiate_ref[...], preferred_element_type=F32
            ).astype(BF16)

    wide = jnp.concatenate([field_ref[one] for one in range(pair)], axis=1)
    pattern = jnp.dot(fold_ref[...], wide, preferred_element_type=F32)
    for one in range(pair):
        mine = pattern[:, one * columns : (one + 1) * columns]
        upper_ref[one] = mine.astype(BF16)
        turned_ref[one] = mine.T.astype(BF16)


def fold(interp_one, radiate, field):
    children, samples1, _ = interp_one.shape
    unknowns = radiate.shape[1]
    parents, width, columns = field.shape
    pair = 2 if parents % 2 == 0 else 1
    return pl.pallas_call(
        fold_kernel,
        grid=(parents // pair,),
        out_shape=(
            jax.ShapeDtypeStruct((samples1, children * unknowns), BF16),
            jax.ShapeDtypeStruct((parents, samples1, columns), BF16),
            jax.ShapeDtypeStruct((parents, columns, samples1), BF16),
        ),
        in_specs=[
            pl.BlockSpec(interp_one.shape, lambda i: (0, 0, 0)),
            pl.BlockSpec(radiate.shape, lambda i: (0, 0)),
            pl.BlockSpec((pair, width, columns), lambda i: (i, 0, 0)),
        ],
        out_specs=(
            pl.BlockSpec((samples1, children * unknowns), lambda i: (0, 0)),
            pl.BlockSpec((pair, samples1, columns), lambda i: (i, 0, 0)),
            pl.BlockSpec((pair, columns, samples1), lambda i: (i, 0, 0)),
        ),
        compiler_params=params(56),
        cost_estimate=cost(3 * 10**9, 6 * 2**20),
        name="fold",
    )(interp_one, radiate, field)


def coarse_kernel(two_ref, upper_ref, out_ref):
    total = jnp.dot(two_ref[0], upper_ref[0], preferred_element_type=F32)
    for child in range(1, two_ref.shape[0]):
        total += jnp.dot(two_ref[child], upper_ref[child], preferred_element_type=F32)
    out_ref[0] = total.astype(BF16)


def coarsen(interp_two, upper):
    children, samples2, samples1 = interp_two.shape
    parents, _, columns = upper.shape
    grand = parents // children
    rows = min(samples2, 256)
    return pl.pallas_call(
        coarse_kernel,
        grid=(samples2 // rows, grand),
        out_shape=jax.ShapeDtypeStruct((grand, samples2, columns), BF16),
        in_specs=[
            pl.BlockSpec((children, rows, samples1), lambda q, g: (0, q, 0)),
            pl.BlockSpec((children, samples1, columns), lambda q, g: (g, 0, 0)),
        ],
        out_specs=pl.BlockSpec((1, rows, columns), lambda q, g: (g, q, 0)),
        compiler_params=params(56),
        cost_estimate=cost(4 * 10**9, 18 * 2**20),
        name="coarsen",
    )(interp_two, upper)


def live_count(source_ref, row):
    total = jnp.int32(0)
    for slot in range(source_ref.shape[1]):
        total += (source_ref[row, slot] >= 0).astype(jnp.int32)
    return total


def list_sum(offset_ref, source_ref, box, shape, weight_at, pattern_at, base):
    unroll = next(n for n in (4, 2, 1) if source_ref.shape[1] % n == 0)

    def add(trip, total):
        for one in range(unroll):
            slot = trip * unroll + one
            named = source_ref[box, slot]
            live = named >= 0
            weight = weight_at(offset_ref[box, slot]) * live.astype(F32)
            total = total + weight * pattern_at(jnp.where(live, named - base, 0))
        return total

    trips = (live_count(source_ref, box) + unroll - 1) // unroll
    return lax.fori_loop(0, trips, add, jnp.zeros(shape, F32))


def level2_kernel(offset_ref, source_ref, table_ref, pattern_ref, out_ref, turned_ref):
    boxes = pattern_ref.shape[0]

    def turn(box, carry):
        turned_ref[box] = pattern_ref[box].astype(F32).T
        return carry

    lax.fori_loop(0, boxes, turn, 0)

    def per_box(box, carry):
        total = list_sum(
            offset_ref, source_ref, box, turned_ref.shape[1:],
            lambda offset: table_ref[pl.ds(offset, 1), :], lambda source: turned_ref[source], 0,
        )
        out_ref[box] = total.astype(BF16)
        return carry

    lax.fori_loop(0, out_ref.shape[0], per_box, 0)


def level2(offset, source, table, pattern):
    boxes, samples, columns = pattern.shape
    return pl.pallas_call(
        level2_kernel,
        out_shape=jax.ShapeDtypeStruct((offset.shape[0], columns, samples), BF16),
        in_specs=[smem(), smem(), vmem(), vmem()],
        out_specs=vmem(),
        scratch_shapes=[pltpu.VMEM((boxes, columns, samples), F32)],
        compiler_params=params(8),
        cost_estimate=cost(3 * 10**9, 2 * 2**20),
        name="level2",
    )(offset, source, table, pattern)


def weighted_lists(pattern, table, offsets, sources):
    live = sources >= 0
    weights = table[offsets] * live[:, :, None].astype(F32)
    picked = pattern[jnp.where(live, sources, 0)]
    return jnp.einsum("cjk,cjkr->ckr", weights, picked, preferred_element_type=F32)


def level1_kernel(
    place_ref, offset_ref, source_ref, table_ref, fold_ref, turned_ref, low_ref, high_ref,
    across_ref, unfold_ref, rim_ref, rows_ref,
):
    step = pl.program_id(0)
    parents, columns, samples1 = turned_ref.shape
    width = rows_ref.shape[2]
    both = jnp.dot(
        fold_ref[...],
        jnp.concatenate([low_ref[0], high_ref[0]], axis=1),
        preferred_element_type=F32,
    )
    rim_ref[step] = both[:, :columns].T.astype(BF16).astype(F32)
    rim_ref[parents + step] = turned_ref[step].astype(F32)
    rim_ref[2 * parents + step] = both[:, columns:].T.astype(BF16).astype(F32)

    @pl.when(step == 0)
    def _():
        for part in range(rows_ref.shape[0]):
            rows_ref[part] = table_ref[:, part * width : (part + 1) * width]
        for first in range(0, fold_ref.shape[1], 128):
            unfold_ref[first : first + 128, :] = fold_ref[:, first : first + 128].T

    @pl.when(step == parents - 1)
    def _():
        def per_box(box, carry):
            for part in range(samples1 // width):
                lanes = slice(part * width, (part + 1) * width)
                across_ref[box, :, lanes] = list_sum(
                    offset_ref, source_ref, box, (columns, width),
                    lambda offset: rows_ref[part, pl.ds(offset, 1), :],
                    lambda source: rim_ref[source, :, lanes],
                    place_ref[0] * parents - parents,
                )
            return carry

        lax.fori_loop(0, parents, per_box, 0)


def level1(place, offset, source, table, folded, turned, low, high):
    parents, columns, samples1 = turned.shape
    around = pl.BlockSpec((1,) + low.shape[1:], lambda i: (i, 0, 0))
    return pl.pallas_call(
        level1_kernel,
        grid=(parents,),
        out_shape=(
            jax.ShapeDtypeStruct((parents, columns, samples1), F32),
            jax.ShapeDtypeStruct((folded.shape[1], folded.shape[0]), BF16),
        ),
        in_specs=[smem()] * 3
        + [
            pl.BlockSpec(table.shape, lambda i: (0, 0)),
            pl.BlockSpec(folded.shape, lambda i: (0, 0)),
            pl.BlockSpec(turned.shape, lambda i: (0, 0, 0)),
            around,
            around,
        ],
        out_specs=(
            pl.BlockSpec((parents, columns, samples1), lambda i: (0, 0, 0)),
            pl.BlockSpec((folded.shape[1], folded.shape[0]), lambda i: (0, 0)),
        ),
        scratch_shapes=[
            pltpu.VMEM((3 * parents, columns, samples1), F32),
            pltpu.VMEM((samples1 // 128, table.shape[0], 128), F32),
        ],
        compiler_params=params(56),
        cost_estimate=cost(8 * 10**9, 14 * 2**20),
        name="level1",
    )(place, offset, source, table, folded, turned, low, high)


def near_kernel(
    place_ref, index_ref, blocks_ref, low_ref, own_ref, high_ref,
    low_other_ref, other_ref, even_ref, odd_ref, mine_ref, theirs_ref, field_ref, sem,
    *, first, count,
):
    step = pl.program_id(0)
    place = place_ref[0]
    boxes, _, columns = own_ref.shape
    chunk, slots = blocks_ref.shape[:2]
    spans = ((first, boxes - first, 0), (0, boxes, 1), (0, first + count, 2))

    def into(ref, side, which):
        start, length, block = spans[which]
        return pltpu.make_async_copy(
            ref.at[pl.ds(start, length)],
            field_ref.at[
                pl.ds(block * boxes + start, length), :, pl.ds(side * columns, columns)
            ],
            sem.at[side, which],
        )

    @pl.when(step == 0)
    def _():
        for which, ref in enumerate((low_ref, own_ref, high_ref)):
            into(ref, 0, which).start()
        into(low_other_ref, 1, 0).start()
        into(other_ref, 1, 1).start()
        for parity, ref in enumerate((even_ref, odd_ref)):

            @pl.when(place % 2 == parity)
            def _():
                into(ref, 1, 2).start()

        for side, refs in enumerate(
            ((low_ref, own_ref, high_ref), (low_other_ref, other_ref, even_ref))
        ):
            for which, ref in enumerate(refs):
                into(ref, side, which).wait()

    base = place * boxes - boxes
    for box in range(chunk):
        row = first + step * chunk + box
        total = None
        for slot in range(0, slots, 2):
            left, right = [], []
            for one in range(slot, min(slot + 2, slots)):
                block = blocks_ref[box, one]
                if one == 0:
                    where = boxes + row
                else:
                    named = index_ref[one, row]
                    live = named >= 0
                    where = jnp.where(live, named - base, boxes)
                    block = jnp.where(live, block, jnp.zeros_like(block))
                left.append(block)
                right.append(field_ref[where])
            part = jnp.dot(
                jnp.concatenate(left, axis=1),
                jnp.concatenate(right, axis=0),
                preferred_element_type=F32,
            )
            total = part if total is None else total + part
        mine_ref[box] = total[:, :columns]
        theirs_ref[box] = total[:, columns:].astype(BF16)


def near(place, index, blocks, low, own, high, low_other, other, even, odd, first, count):
    boxes, unknowns, columns = own.shape
    _, slots, rows, _ = blocks.shape
    chunk = min(8, count)
    hbm = pl.BlockSpec(memory_space=pl.ANY)
    return pl.pallas_call(
        functools.partial(near_kernel, first=first, count=count),
        grid=(count // chunk,),
        out_shape=(
            jax.ShapeDtypeStruct((count, rows, columns), F32),
            jax.ShapeDtypeStruct((count, rows, columns), BF16),
        ),
        in_specs=[
            smem(),
            smem(),
            pl.BlockSpec((chunk, slots, rows, unknowns), lambda i: (first // chunk + i, 0, 0, 0)),
        ]
        + [hbm] * 7,
        out_specs=(pl.BlockSpec((chunk, rows, columns), lambda i: (i, 0, 0)),) * 2,
        scratch_shapes=[
            pltpu.VMEM((3 * boxes, unknowns, 2 * columns), BF16),
            pltpu.SemaphoreType.DMA((2, 3)),
        ],
        compiler_params=params(56),
        cost_estimate=cost(count * 2 * 10**8, 14 * 2**20 + count * 10**5),
    )(place, index, blocks, low, own, high, low_other, other, even, odd)


def part_index(which, per):
    return lambda i: (jnp.clip(i - which * per, 0, per - 1), 0, 0)


def down_kernel(place_ref, sigma_ref, inc_ref, two_ref, across_ref, unfold_ref, field_ref, *rest, children, pair, parts, shifts):
    near_refs, (out_ref, flat_ref, local_ref) = rest[:parts], rest[parts:]
    chunks, columns, lanes = inc_ref.shape[1:]
    step = pl.program_id(0)
    span_of = pl.num_programs(0) // parts

    @pl.when(step % children == 0)
    def _():
        for one in range(chunks):
            flat_ref[:, one * lanes : (one + 1) * lanes] = inc_ref[0, one]

    down = jnp.dot(flat_ref[...], two_ref[0], preferred_element_type=F32)
    local_ref[pl.ds((step % pair) * columns, columns), :] = (down + across_ref[0]).astype(BF16)

    @pl.when(step % pair == pair - 1)
    def _():
        far = lax.dot_general(unfold_ref[...], local_ref[...], NT, preferred_element_type=F32)
        boxes, unknowns, _ = out_ref.shape
        per = boxes // pair
        half = unknowns // 2
        re, im = sigma_ref[0, 0], sigma_ref[0, 1]
        for one in range(pair):
            mine = far[:, one * columns : (one + 1) * columns].reshape(per, unknowns, columns)
            span = slice(one * per, (one + 1) * per)
            real = field_ref[span, :half, :].astype(F32)
            imag = field_ref[span, half:, :].astype(F32)
            out_ref[span, :half, :] = mine[:, :half] - (re * real - im * imag)
            out_ref[span, half:, :] = mine[:, half:] - (re * imag + im * real)
        rows = near_refs[0].shape[1]
        for shift in range(shifts):
            for part, near_ref in enumerate(near_refs):

                @pl.when((place_ref[1] == shift) & (step // span_of == part))
                def _():
                    out_ref[:, shift * rows : (shift + 1) * rows, :] += near_ref[...]


def downward(place, sigma, inc, interp_two, across, unfold, field, near_parts, shifts):
    grand, chunks, columns, lanes = inc.shape
    children, samples2, samples1 = interp_two.shape
    boxes, unknowns, _ = field.shape
    rows = near_parts[0].shape[1]
    parts = len(near_parts)
    pair = 2 if children % 2 == 0 else 1
    per = pair * (boxes // across.shape[0])
    each = boxes // per // parts
    return pl.pallas_call(
        functools.partial(down_kernel, children=children, pair=pair, parts=parts, shifts=shifts),
        grid=(grand * children,),
        out_shape=jax.ShapeDtypeStruct((boxes, unknowns, columns), F32),
        in_specs=[
            smem(),
            smem(),
            pl.BlockSpec((1, chunks, columns, lanes), lambda c: (c // children, 0, 0, 0)),
            pl.BlockSpec((1, samples2, samples1), lambda c: (c % children, 0, 0)),
            pl.BlockSpec((1, columns, samples1), lambda c: (c, 0, 0)),
            pl.BlockSpec(unfold.shape, lambda c: (0, 0)),
            pl.BlockSpec((per, unknowns, columns), lambda c: (c // pair, 0, 0)),
        ]
        + [
            pl.BlockSpec((per, rows, columns), lambda c, part=part: part_index(part, each)(c // pair))
            for part in range(parts)
        ],
        out_specs=pl.BlockSpec((per, unknowns, columns), lambda c: (c // pair, 0, 0)),
        scratch_shapes=[
            pltpu.VMEM((columns, chunks * lanes), BF16),
            pltpu.VMEM((pair * columns, samples1), BF16),
        ],
        compiler_params=params(56),
        cost_estimate=cost(6 * 10**9, 30 * 2**20),
        name="downward",
    )(place, sigma, inc, interp_two, across, unfold, field, *near_parts)


def join_kernel(place_ref, total_ref, *rest, parts):
    part_refs, out_ref = rest[:parts], rest[parts]
    each = pl.num_programs(0) // parts
    for part, part_ref in enumerate(part_refs):

        @pl.when(pl.program_id(0) // each == part)
        def _():
            out_ref[...] = total_ref[...] + part_ref[...].astype(F32)


def join(place, total, arrived):
    boxes, _, columns = total.shape
    count, rows, _ = arrived[0].shape
    parts = len(arrived)
    step = min(16, count)
    each = count // step
    half = pl.BlockSpec((step, rows, columns), lambda i, place_ref: (i, 1 - place_ref[1], 0))
    return pl.pallas_call(
        functools.partial(join_kernel, parts=parts),
        grid_spec=pltpu.PrefetchScalarGridSpec(
            num_scalar_prefetch=1,
            grid=(boxes // step,),
            in_specs=[half]
            + [
                pl.BlockSpec((step, rows, columns), lambda i, place_ref, part=part: part_index(part, each)(i))
                for part in range(parts)
            ],
            out_specs=half,
        ),
        out_shape=jax.ShapeDtypeStruct(total.shape, F32),
        input_output_aliases={1: 0},
        compiler_params=params(10),
        cost_estimate=cost(10**7, 5 * 2**20),
        name="join",
    )(place, total, *arrived)


def body(
    vectors, sigma, near_blocks, near_index, radiate, interp_one, interp_two, trans_one,
    level1_source, level1_offset, trans_two, level2_source, level2_offset,
):
    field = vectors[0]
    boxes, unknowns, columns = field.shape
    children, _, _ = interp_one.shape
    samples2 = interp_two.shape[1]
    parents = boxes // children
    grand = parents // children
    count = lax.axis_size("box")
    shifts = lax.axis_size("shift")
    place = jnp.stack([lax.axis_index("box"), lax.axis_index("shift")]).astype(jnp.int32)

    up = [(i, i + 1) for i in range(count - 1)]
    down = [(i + 1, i) for i in range(count - 1)]
    swap = [(s, shifts - 1 - s) for s in range(shifts)]
    pair_down = [(i + 1, i) for i in range(0, count - 1, 2)]
    odd_swap = [
        (i * shifts + s, i * shifts + shifts - 1 - s) for i in range(1, count, 2) for s in range(shifts)
    ]

    other = lax.ppermute(field, "shift", swap)
    high = lax.ppermute(field, "box", down)
    low = lax.ppermute(field, "box", up)

    folded, upper, turned = fold(
        interp_one, radiate, field.reshape(parents, children * unknowns, columns)
    )
    coarse = coarsen(interp_two, upper)
    chunk = samples2 // count
    pieces = coarse.reshape(grand, count, chunk, columns).swapaxes(0, 1)
    spread = lax.all_to_all(pieces, "box", split_axis=0, concat_axis=0, tiled=True)
    spread = spread.reshape(count * grand, chunk, columns)
    if chunk % 128 == 0:
        inc = level2(level2_offset, level2_source, trans_two, spread)
        inc = lax.all_to_all(
            inc.reshape(count, grand, columns, chunk), "box", split_axis=0, concat_axis=0, tiled=True
        ).swapaxes(0, 1)
    else:
        inc = weighted_lists(spread, trans_two, level2_offset, level2_source).astype(BF16)
        inc = lax.all_to_all(
            inc.reshape(count, grand, chunk, columns), "box", split_axis=0, concat_axis=0, tiled=True
        ).swapaxes(0, 1)
        inc = inc.reshape(grand, samples2 // 128, 128, columns).swapaxes(2, 3)

    relayed, other = lax.optimization_barrier((high, other))
    high_odd = lax.ppermute(relayed, ("box", "shift"), odd_swap)
    low_other = lax.ppermute(other, "box", up)
    high_even = lax.ppermute(other, "box", pair_down)

    wide = (parents, children * unknowns, columns)
    across, unfold = level1(
        place, level1_offset, level1_source, trans_one, folded, turned,
        low.reshape(wide), high.reshape(wide),
    )
    low, across = lax.optimization_barrier((low, across))
    splits = 2
    part = boxes // splits
    near_parts, arrived = [], []
    for one in range(splits):
        mine, theirs = near(
            place, near_index.T, near_blocks, low, field, high,
            low_other, other, high_even, high_odd, one * part, part,
        )
        near_parts.append(mine)
        arrived.append(lax.ppermute(theirs, "shift", swap))

    total = downward(place, sigma, inc, interp_two, across, unfold, field, near_parts, shifts)
    total = join(place, total, arrived)
    return total[None]


def solution(mesh):
    in_specs = (
        P("shift", "box", None, None),
        P("shift", None),
        P("box", None, "shift", None),
        P("box", None),
        P(),
        P(),
        P(),
        P(),
        P("box", None),
        P("box", None),
        P(None, "box"),
        P(),
        P(),
    )
    out_specs = P("shift", "box", None, None)

    return jax.shard_map(body, mesh=mesh, in_specs=in_specs, out_specs=out_specs, check_vma=False)
```

profile of v0, /device:TPU:0, one launch (start us, length us, event | category | flops | bytes accessed | tf_op | source)
XLA Modules:
  0.0 160.9 jit_solution(14797700033908080916)
XLA Ops:
  0.0 3.0 %collective-permute-start.2 = (bf16[64,128,128]{2,1,0:T(8,128)(2,1)}, bf16[64,128,128]{2,1,0:T(8,128)(2,1)S(1)}, u32[]{:S(2)}, u32[]{:S(2)}) collective-permute-start(bf16[64,128,128]{2,1,0:T(8,128)(2,1)} %bitcast.18), channel_id=1, source_target_pairs={{0,1},{1,0},{2,3},{3,2},{4,5},{5,4},{6,7},{7,6},{8,9},{9,8},{10,11... | collective-permute-start | bytes 6291464 | tf_op jit(solution)/shard_map/ppermute | solution.py:474
  3.0 1.3 collective-permute-start.1
  4.3 4.4 %collective-permute-start = (bf16[64,128,128]{2,1,0:T(8,128)(2,1)}, bf16[64,128,128]{2,1,0:T(8,128)(2,1)}, u32[]{:S(2)}, u32[]{:S(2)}) collective-permute-start(bf16[64,128,128]{2,1,0:T(8,128)(2,1)} %bitcast.20), channel_id=1, source_target_pairs={{0,2},{2,4},{4,6},{6,8},{8,10},{10,12},{12,14},{14,16},{16,18},{18... | collective-permute-start | bytes 6291464 | tf_op jit(solution)/shard_map/ppermute | solution.py:476
  8.7 5.4 %fold.1 = (bf16[512,1024]{1,0:T(8,128)(2,1)}, bf16[8,512,128]{2,1,0:T(8,128)(2,1)}, bf16[8,128,512]{2,1,0:T(8,128)(2,1)}) custom-call(bf16[8,512,128]{2,1,0:T(8,128)(2,1)} %one_ref.1, bf16[128,128]{1,0:T(8,128)(2,1)} %radiate_ref.1, bf16[8,1024,128]{2,1,0:T(8,128)(2,1)} %bitcast.21), custom_call_target="tpu_custom_call" | custom-call | flops 3000000000 | bytes 6291456 | tf_op jit(solution)/shard_map/fold/pallas_call | solution.py:57
  14.1 34.8 %collective-permute-done.2.other_ref = bf16[64,128,128]{2,1,0:T(8,128)(2,1)S(1)} collective-permute-done((bf16[64,128,128]{2,1,0:T(8,128)(2,1)}, bf16[64,128,128]{2,1,0:T(8,128)(2,1)S(1)}, u32[]{:S(2)}, u32[]{:S(2)}) %collective-permute-start.2) | collective-permute-done | bytes 2097184 | tf_op jit(solution)/shard_map/ppermute | solution.py:474
  48.8 0.0 collective-permute-done.1.high_ref
  48.8 1.3 collective-permute-start.4
  50.1 5.7 %collective-permute-start.3 = (bf16[64,128,128]{2,1,0:T(8,128)(2,1)S(1)}, bf16[64,128,128]{2,1,0:T(8,128)(2,1)}, u32[]{:S(2)}, u32[]{:S(2)}) collective-permute-start(bf16[64,128,128]{2,1,0:T(8,128)(2,1)S(1)} %collective-permute-done.2.other_ref), channel_id=1, source_target_pairs={{0,2},{2,4},{4,6},{6,8},{8,10},{10,12},{12,14},{14,16},{16,18},{18... | collective-permute-start | bytes 6291464 | tf_op jit(solution)/shard_map/ppermute | solution.py:500
  55.9 2.1 %collective-permute-start.5 = (bf16[64,128,128]{2,1,0:T(8,128)(2,1)}, bf16[64,128,128]{2,1,0:T(8,128)(2,1)}, u32[]{:S(2)}, u32[]{:S(2)}) collective-permute-start(bf16[64,128,128]{2,1,0:T(8,128)(2,1)} %collective-permute-done.1.high_ref), channel_id=1, source_target_pairs={{2,3},{3,2},{6,7},{7,6},{10,11},{11,10},{14,15},{15,14},{18,19},{1... | collective-permute-start | bytes 6291464 | tf_op jit(solution)/shard_map/ppermute | solution.py:499
  57.9 11.4 %coarsen.1 = bf16[1,2048,128]{2,1,0:T(8,128)(2,1)} custom-call(bf16[8,2048,512]{2,1,0:T(8,128)(2,1)} %two_ref.3, bf16[8,512,128]{2,1,0:T(8,128)(2,1)} %get-tuple-element.18.upper_ref), custom_call_target="tpu_custom_call" | custom-call | flops 4000000000 | bytes 18874368 | tf_op jit(solution)/shard_map/coarsen/pallas_call | solution.py:93
  69.3 7.0 %all-to-all-start = ((bf16[16,1,128,128]{3,2,1,0:T(8,128)(2,1)}), bf16[16,1,128,128]{3,2,1,0:T(8,128)(2,1)S(1)}, u32[]{:S(2)}, u32[]{:S(2)}) async-start(bf16[16,1,128,128]{3,2,1,0:T(8,128)(2,1)} %bitcast.25), calls=%async_computation | async-start | bytes 1048576 | tf_op jit(solution)/shard_map/all_to_all | solution.py:484
  76.3 0.7 pad_add_fusion.place_ref
  77.0 13.6 %all-to-all-done = bf16[16,1,128,128]{3,2,1,0:T(8,128)(2,1)S(1)} async-done(((bf16[16,1,128,128]{3,2,1,0:T(8,128)(2,1)}), bf16[16,1,128,128]{3,2,1,0:T(8,128)(2,1)S(1)}, u32[]{:S(2)}, u32[]{:S(2)}) %all-to-all-start) | async-done | bytes 524320 | tf_op jit(solution)/shard_map/all_to_all | solution.py:484
  90.6 7.1 %level2.1 = bf16[16,128,128]{2,1,0:T(8,128)(2,1)} custom-call(s32[16,32]{1,0:T(8,128)S(1)} %copy-done.2, s32[16,32]{1,0:T(8,128)S(1)} %copy-done.3, f32[316,128]{1,0:T(8,128)S(1)} %copy-done.1, bf16[16,128,128]{2,1,0:T(8,128)(2,1)S(1)} %bitcast.16), custom_call_target="tpu_custom_call" | custom-call | flops 3000000000 | bytes 2097152 | tf_op jit(solution)/shard_map/level2/pallas_call | solution.py:153
  97.7 6.8 %all-to-all-start.1 = ((bf16[16,1,128,128]{3,2,1,0:T(8,128)(2,1)}), bf16[16,1,128,128]{3,2,1,0:T(8,128)(2,1)S(1)}, u32[]{:S(2)}, u32[]{:S(2)}) async-start(bf16[16,1,128,128]{3,2,1,0:T(8,128)(2,1)} %bitcast.7), calls=%async_computation.1 | async-start | bytes 1048576 | tf_op jit(solution)/shard_map/all_to_all | solution.py:488
  104.5 0.0 collective-permute-done.low_ref
  104.5 14.9 %level1.1 = (f32[8,128,512]{2,1,0:T(8,128)}, bf16[1024,512]{1,0:T(8,128)(2,1)}) custom-call(s32[2]{0:T(128)} %pad_add_fusion.place_ref, s32[8,16]{1,0:T(8,128)} %offset_ref.3, s32[8,16]{1,0:T(8,128)} %source_ref.3, f32[316,512]{1,0:T(8,128)} %table_ref.3, bf16[512,1024]{1,0:T(8,128)(2,1)} %get-tuple-element.19.fold_ref, ...), custom_call_target="tpu_custom_call" | custom-call | flops 8000000000 | bytes 14680064 | tf_op jit(solution)/shard_map/level1/pallas_call | solution.py:214
  119.4 9.5 %shard_map.128 = (f32[32,64,128]{2,1,0:T(8,128)}, bf16[32,64,128]{2,1,0:T(8,128)(2,1)}) custom-call(s32[2]{0:T(128)} %pad_add_fusion.place_ref, s32[6,64]{1,0:T(8,128)} %bitcast.26, bf16[64,6,64,128]{3,2,1,0:T(8,128)(2,1)} %blocks_ref.3, bf16[64,128,128]{2,1,0:T(8,128)(2,1)} %collective-permute-done.low_ref, bf16[64,128,128]{2,1,0:T(8,128)(2,1)} %bitcast.22, ...), custom_call_target="tpu_custom_call" | custom-call | flops 6400000000 | bytes 17880064 | tf_op jit(solution)/shard_map/pallas_call | solution.py:314
  128.9 0.6 collective-permute-start.7
  129.5 9.5 %shard_map.127 = (f32[32,64,128]{2,1,0:T(8,128)}, bf16[32,64,128]{2,1,0:T(8,128)(2,1)}) custom-call(s32[2]{0:T(128)} %pad_add_fusion.place_ref, s32[6,64]{1,0:T(8,128)} %bitcast.27, bf16[64,6,64,128]{3,2,1,0:T(8,128)(2,1)} %blocks_ref.3, bf16[64,128,128]{2,1,0:T(8,128)(2,1)} %collective-permute-done.low_ref, bf16[64,128,128]{2,1,0:T(8,128)(2,1)} %bitcast.23, ...), custom_call_target="tpu_custom_call" | custom-call | flops 6400000000 | bytes 17880064 | tf_op jit(solution)/shard_map/pallas_call | solution.py:314
  139.0 1.5 collective-permute-start.6
  140.5 0.8 copy-done.4
  141.3 15.1 %downward.1.total_ref = f32[64,128,128]{2,1,0:T(8,128)} custom-call(s32[2]{0:T(128)} %pad_add_fusion.place_ref, f32[1,2]{1,0:T(1,128)} %sigma_ref.1, bf16[1,16,128,128]{3,2,1,0:T(8,128)(2,1)} %bitcast.17, bf16[8,2048,512]{2,1,0:T(8,128)(2,1)} %two_ref.3, f32[8,128,512]{2,1,0:T(8,128)} %get-tuple-element.22.across_ref, ...), custom_call_target="tpu_custom_call" | custom-call | flops 6000000000 | bytes 31457280 | tf_op jit(solution)/shard_map/downward/pallas_call | solution.py:387
  156.5 4.4 %join.1 = f32[64,128,128]{2,1,0:T(8,128)} custom-call(s32[2]{0:T(128)S(1)} %copy-done, f32[64,128,128]{2,1,0:T(8,128)} %downward.1.total_ref, bf16[32,64,128]{2,1,0:T(8,128)(2,1)S(1)} %collective-permute-done.6.rest_0_, bf16[32,64,128]{2,1,0:T(8,128)(2,1)S(1)} %collective-permute-done.7.rest_1_), custom_call_target="tpu_custom_call", output_to_operand_aliasing={{}: (1, {})} | custom-call | flops 10000000 | bytes 5242880 | tf_op jit(solution)/shard_map/join/pallas_call | solution.py:432
  (17 shorter events, 0.0 us)
Async XLA Ops:
  0.0 48.8 %collective-permute-start.2 = (bf16[64,128,128]{2,1,0:T(8,128)(2,1)}, bf16[64,128,128]{2,1,0:T(8,128)(2,1)S(1)}, u32[]{:S(2)}, u32[]{:S(2)}) collective-permute-start(bf16[64,128,128]{2,1,0:T(8,128)(2,1)} %bitcast.18), channel_id=1, source_target_pairs={{0,1},{1,0},{2,3},{3,2},{4,5},{5,4},{6,7},{7,6},{8,9},{9,8},{10,11... | collective-permute-start | bytes 6291464 | tf_op jit(solution)/shard_map/ppermute | solution.py:474
  3.0 45.8 %collective-permute-start.1 = (bf16[64,128,128]{2,1,0:T(8,128)(2,1)}, bf16[64,128,128]{2,1,0:T(8,128)(2,1)}, u32[]{:S(2)}, u32[]{:S(2)}) collective-permute-start(bf16[64,128,128]{2,1,0:T(8,128)(2,1)} %bitcast.19), channel_id=1, source_target_pairs={{2,0},{4,2},{6,4},{8,6},{10,8},{12,10},{14,12},{16,14},{18,16},{20... | collective-permute-start | bytes 6291464 | tf_op jit(solution)/shard_map/ppermute | solution.py:475
  4.3 100.2 %collective-permute-start = (bf16[64,128,128]{2,1,0:T(8,128)(2,1)}, bf16[64,128,128]{2,1,0:T(8,128)(2,1)}, u32[]{:S(2)}, u32[]{:S(2)}) collective-permute-start(bf16[64,128,128]{2,1,0:T(8,128)(2,1)} %bitcast.20), channel_id=1, source_target_pairs={{0,2},{2,4},{4,6},{6,8},{8,10},{10,12},{12,14},{14,16},{16,18},{18... | collective-permute-start | bytes 6291464 | tf_op jit(solution)/shard_map/ppermute | solution.py:476
  48.8 20.5 %copy-start.5 = (bf16[64,128,128]{2,1,0:T(8,128)(2,1)}, bf16[64,128,128]{2,1,0:T(8,128)(2,1)S(1)}, u32[]{:S(2)}) copy-start(bf16[64,128,128]{2,1,0:T(8,128)(2,1)S(1)} %collective-permute-done.2.other_ref) | copy-start | bytes 6291460
  48.8 70.5 %collective-permute-start.4 = (bf16[64,128,128]{2,1,0:T(8,128)(2,1)S(1)}, bf16[64,128,128]{2,1,0:T(8,128)(2,1)}, u32[]{:S(2)}, u32[]{:S(2)}) collective-permute-start(bf16[64,128,128]{2,1,0:T(8,128)(2,1)S(1)} %collective-permute-done.2.other_ref), channel_id=1, source_target_pairs={{2,0},{6,4},{10,8},{14,12},{18,16},{22,20},{26,24},{30,28},{3,1},{... | collective-permute-start | bytes 6291464 | tf_op jit(solution)/shard_map/ppermute | solution.py:501
  50.1 69.2 %collective-permute-start.3 = (bf16[64,128,128]{2,1,0:T(8,128)(2,1)S(1)}, bf16[64,128,128]{2,1,0:T(8,128)(2,1)}, u32[]{:S(2)}, u32[]{:S(2)}) collective-permute-start(bf16[64,128,128]{2,1,0:T(8,128)(2,1)S(1)} %collective-permute-done.2.other_ref), channel_id=1, source_target_pairs={{0,2},{2,4},{4,6},{6,8},{8,10},{10,12},{12,14},{14,16},{16,18},{18... | collective-permute-start | bytes 6291464 | tf_op jit(solution)/shard_map/ppermute | solution.py:500
  55.9 63.5 %collective-permute-start.5 = (bf16[64,128,128]{2,1,0:T(8,128)(2,1)}, bf16[64,128,128]{2,1,0:T(8,128)(2,1)}, u32[]{:S(2)}, u32[]{:S(2)}) collective-permute-start(bf16[64,128,128]{2,1,0:T(8,128)(2,1)} %collective-permute-done.1.high_ref), channel_id=1, source_target_pairs={{2,3},{3,2},{6,7},{7,6},{10,11},{11,10},{14,15},{15,14},{18,19},{1... | collective-permute-start | bytes 6291464 | tf_op jit(solution)/shard_map/ppermute | solution.py:499
  57.9 32.7 %copy-start.1 = (f32[316,128]{1,0:T(8,128)S(1)}, f32[316,128]{1,0:T(8,128)}, u32[]{:S(2)}) copy-start(f32[316,128]{1,0:T(8,128)} %table_ref.2) | copy-start | bytes 485380
  57.9 32.7 %copy-start.2 = (s32[16,32]{1,0:T(8,128)S(1)}, s32[16,32]{1,0:T(8,128)}, u32[]{:S(2)}) copy-start(s32[16,32]{1,0:T(8,128)} %offset_ref.2) | copy-start | bytes 6148
  57.9 32.7 %copy-start.3 = (s32[16,32]{1,0:T(8,128)S(1)}, s32[16,32]{1,0:T(8,128)}, u32[]{:S(2)}) copy-start(s32[16,32]{1,0:T(8,128)} %source_ref.2) | copy-start | bytes 6148
  69.3 21.2 %all-to-all-start = ((bf16[16,1,128,128]{3,2,1,0:T(8,128)(2,1)}), bf16[16,1,128,128]{3,2,1,0:T(8,128)(2,1)S(1)}, u32[]{:S(2)}, u32[]{:S(2)}) async-start(bf16[16,1,128,128]{3,2,1,0:T(8,128)(2,1)} %bitcast.25), calls=%async_computation | async-start | bytes 1048576 | tf_op jit(solution)/shard_map/all_to_all | solution.py:484
  97.7 42.8 %all-to-all-start.1 = ((bf16[16,1,128,128]{3,2,1,0:T(8,128)(2,1)}), bf16[16,1,128,128]{3,2,1,0:T(8,128)(2,1)S(1)}, u32[]{:S(2)}, u32[]{:S(2)}) async-start(bf16[16,1,128,128]{3,2,1,0:T(8,128)(2,1)} %bitcast.7), calls=%async_computation.1 | async-start | bytes 1048576 | tf_op jit(solution)/shard_map/all_to_all | solution.py:488
  128.9 27.6 %collective-permute-start.7 = (bf16[32,64,128]{2,1,0:T(8,128)(2,1)}, bf16[32,64,128]{2,1,0:T(8,128)(2,1)S(1)}, u32[]{:S(2)}, u32[]{:S(2)}) collective-permute-start(bf16[32,64,128]{2,1,0:T(8,128)(2,1)} %get-tuple-element.30), channel_id=1, source_target_pairs={{0,1},{1,0},{2,3},{3,2},{4,5},{5,4},{6,7},{7,6},{8,9},{9,8},{10,11... | collective-permute-start | bytes 1572872 | tf_op jit(solution)/shard_map/ppermute | solution.py:518
  139.0 17.5 %collective-permute-start.6 = (bf16[32,64,128]{2,1,0:T(8,128)(2,1)}, bf16[32,64,128]{2,1,0:T(8,128)(2,1)S(1)}, u32[]{:S(2)}, u32[]{:S(2)}) collective-permute-start(bf16[32,64,128]{2,1,0:T(8,128)(2,1)} %get-tuple-element.29), channel_id=1, source_target_pairs={{0,1},{1,0},{2,3},{3,2},{4,5},{5,4},{6,7},{7,6},{8,9},{9,8},{10,11... | collective-permute-start | bytes 1572872 | tf_op jit(solution)/shard_map/ppermute | solution.py:518
  140.5 0.8 copy-start.4
  141.3 15.2 %copy-start = (s32[2]{0:T(128)S(1)}, s32[2]{0:T(128)}, u32[]{:S(2)}) copy-start(s32[2]{0:T(128)} %pad_add_fusion.place_ref) | copy-start | bytes 28
where the time goes:
time: 162 us; the launch traced here: 161 us
  Pallas kernels  77.3 us (48%)
  waiting for transfers between devices  48.4 us (30%)
  starting transfers between devices  33.6 us (21%)
    ppermute x1, waiting for transfers between devices, body(): other = lax.ppermute(field, 'shift', swap)  34.8 us
    pallas_call x2, Pallas kernels, near(): pl.pallas_call(functools.partial(near_kernel, first=first, count=count),...  19 us
    pallas_call x1, Pallas kernels, downward(): pl.pallas_call(functools.partial(down_kernel, children=children, pair=pai...  15.1 us
    pallas_call x1, Pallas kernels, level1(): pl.pallas_call(level1_kernel, grid=(parents,), out_shape=(jax.ShapeDtypeS...  14.9 us
    all_to_all x1, waiting for transfers between devices, body(): lax.all_to_all(pieces, 'box', split_axis=0, concat_axis=0, tiled=True)  13.6 us
    pallas_call x1, Pallas kernels, coarsen(): pl.pallas_call(coarse_kernel, grid=(samples2 // rows, grand), out_shape=j...  11.4 us
    pallas_call x1, Pallas kernels, level2(): pl.pallas_call(level2_kernel, out_shape=jax.ShapeDtypeStruct((offset.shap...  7.1 us
    all_to_all x1, starting transfers between devices, body(): lax.all_to_all(pieces, 'box', split_axis=0, concat_axis=0, tiled=True)  6.97 us
  transfers between devices with their start and end apart: 10, of which 2 were waited for; matrix products, arithmetic and copies ran while one was open for 0% of the time, Pallas kernels for 45%

commit v1 on v0

--- a/solution.py
+++ b/solution.py
@@ -241,43 +241,59 @@
 
 
 def near_kernel(
-    place_ref, index_ref, blocks_ref, low_ref, own_ref, high_ref,
-    low_other_ref, other_ref, even_ref, odd_ref, mine_ref, theirs_ref, field_ref, sem,
-    *, first, count,
+    place_ref, index_ref, blocks_ref, low_ref, own_ref, high_ref, odd_ref, *rest, first, count, cuts,
 ):
+    swapped_refs, piece_refs, even_refs = rest[: cuts[0]], rest[cuts[0] : cuts[1]], rest[cuts[1] : -4]
+    mine_ref, theirs_ref, field_ref, sem = rest[-4:]
     step = pl.program_id(0)
     place = place_ref[0]
     boxes, _, columns = own_ref.shape
     chunk, slots = blocks_ref.shape[:2]
-    spans = ((first, boxes - first, 0), (0, boxes, 1), (0, first + count, 2))
-
-    def into(ref, side, which):
-        start, length, block = spans[which]
+
+    def into(ref, source, length, target, side, lane):
         return pltpu.make_async_copy(
-            ref.at[pl.ds(start, length)],
-            field_ref.at[
-                pl.ds(block * boxes + start, length), :, pl.ds(side * columns, columns)
-            ],
-            sem.at[side, which],
+            ref.at[pl.ds(source, length)],
+            field_ref.at[pl.ds(target, length), :, pl.ds(side * columns, columns)],
+            sem.at[lane],
         )
+
+    copies = [
+        into(low_ref, first, boxes - first, first, 0, 0),
+        into(own_ref, 0, boxes, boxes, 0, 1),
+        into(high_ref, 0, first + count, 2 * boxes, 0, 2),
+    ]
+    lane = 3
+    for refs, target in ((swapped_refs, boxes), (piece_refs, first)):
+        for one, ref in enumerate(refs):
+            length = ref.shape[0]
+            copies.append(into(ref, 0, length, target + one * length, 1, lane))
+            lane += 1
+    even = []
+    for one, ref in enumerate(even_refs):
+        length = ref.shape[0]
+        even.append(into(ref, 0, length, 2 * boxes + one * length, 1, lane))
+        lane += 1
+    odd = into(odd_ref, 0, first + count, 2 * boxes, 1, lane)
 
     @pl.when(step == 0)
     def _():
-        for which, ref in enumerate((low_ref, own_ref, high_ref)):
-            into(ref, 0, which).start()
-        into(low_other_ref, 1, 0).start()
-        into(other_ref, 1, 1).start()
-        for parity, ref in enumerate((even_ref, odd_ref)):
-
-            @pl.when(place % 2 == parity)
-            def _():
-                into(ref, 1, 2).start()
-
-        for side, refs in enumerate(
-            ((low_ref, own_ref, high_ref), (low_other_ref, other_ref, even_ref))
-        ):
-            for which, ref in enumerate(refs):
-                into(ref, side, which).wait()
+        for copy in copies:
+            copy.start()
+
+        @pl.when(place % 2 == 0)
+        def _():
+            for copy in even:
+                copy.start()
+            for copy in even:
+                copy.wait()
+
+        @pl.when(place % 2 == 1)
+        def _():
+            odd.start()
+            odd.wait()
+
+        for copy in copies:
+            copy.wait()
 
     base = place * boxes - boxes
     for box in range(chunk):
@@ -306,13 +322,17 @@
         theirs_ref[box] = total[:, columns:].astype(BF16)
 
 
-def near(place, index, blocks, low, own, high, low_other, other, even, odd, first, count):
+def near(place, index, blocks, low, own, high, odd, swapped, pieces, evens, first, count):
     boxes, unknowns, columns = own.shape
     _, slots, rows, _ = blocks.shape
     chunk = min(8, count)
+    lanes = len(swapped) + len(pieces) + len(evens)
     hbm = pl.BlockSpec(memory_space=pl.ANY)
     return pl.pallas_call(
-        functools.partial(near_kernel, first=first, count=count),
+        functools.partial(
+            near_kernel, first=first, count=count,
+            cuts=(len(swapped), len(swapped) + len(pieces)),
+        ),
         grid=(count // chunk,),
         out_shape=(
             jax.ShapeDtypeStruct((count, rows, columns), F32),
@@ -323,15 +343,15 @@
             smem(),
             pl.BlockSpec((chunk, slots, rows, unknowns), lambda i: (first // chunk + i, 0, 0, 0)),
         ]
-        + [hbm] * 7,
+        + [hbm] * (4 + lanes),
         out_specs=(pl.BlockSpec((chunk, rows, columns), lambda i: (i, 0, 0)),) * 2,
         scratch_shapes=[
             pltpu.VMEM((3 * boxes, unknowns, 2 * columns), BF16),
-            pltpu.SemaphoreType.DMA((2, 3)),
+            pltpu.SemaphoreType.DMA((4 + lanes,)),
         ],
         compiler_params=params(56),
         cost_estimate=cost(count * 2 * 10**8, 14 * 2**20 + count * 10**5),
-    )(place, index, blocks, low, own, high, low_other, other, even, odd)
+    )(place, index, blocks, low, own, high, odd, *swapped, *pieces, *evens)
 
 
 def part_index(which, per):
@@ -471,7 +491,13 @@
         (i * shifts + s, i * shifts + shifts - 1 - s) for i in range(1, count, 2) for s in range(shifts)
     ]
 
-    other = lax.ppermute(field, "shift", swap)
+    splits = 2
+    part = boxes // splits
+    swapped = [None] * splits
+    for one in reversed(range(splits)):
+        swapped[one] = lax.ppermute(
+            lax.slice_in_dim(field, one * part, (one + 1) * part, axis=0), "shift", swap
+        )
     high = lax.ppermute(field, "box", down)
     low = lax.ppermute(field, "box", up)
 
@@ -487,18 +513,22 @@
         inc = level2(level2_offset, level2_source, trans_two, spread)
         inc = lax.all_to_all(
             inc.reshape(count, grand, columns, chunk), "box", split_axis=0, concat_axis=0, tiled=True
-        ).swapaxes(0, 1)
+        )
+        inc = inc.swapaxes(0, 1)
     else:
         inc = weighted_lists(spread, trans_two, level2_offset, level2_source).astype(BF16)
         inc = lax.all_to_all(
             inc.reshape(count, grand, chunk, columns), "box", split_axis=0, concat_axis=0, tiled=True
-        ).swapaxes(0, 1)
+        )
+        inc = inc.swapaxes(0, 1)
         inc = inc.reshape(grand, samples2 // 128, 128, columns).swapaxes(2, 3)
 
-    relayed, other = lax.optimization_barrier((high, other))
-    high_odd = lax.ppermute(relayed, ("box", "shift"), odd_swap)
-    low_other = lax.ppermute(other, "box", up)
-    high_even = lax.ppermute(other, "box", pair_down)
+    pieces, evens = [], []
+    for one in range(splits):
+        pieces.append(lax.ppermute(swapped[one], "box", up))
+    for one in range(splits):
+        evens.append(lax.ppermute(swapped[one], "box", pair_down))
+    high_odd = lax.ppermute(high, ("box", "shift"), odd_swap)
 
     wide = (parents, children * unknowns, columns)
     across, unfold = level1(
@@ -506,16 +536,14 @@
         low.reshape(wide), high.reshape(wide),
     )
     low, across = lax.optimization_barrier((low, across))
-    splits = 2
-    part = boxes // splits
-    near_parts, arrived = [], []
-    for one in range(splits):
+    near_parts, arrived = [None] * splits, [None] * splits
+    for one in reversed(range(splits)):
         mine, theirs = near(
-            place, near_index.T, near_blocks, low, field, high,
-            low_other, other, high_even, high_odd, one * part, part,
+            place, near_index.T, near_blocks, low, field, high, high_odd,
+            swapped, pieces[one:], evens[: one + 1], one * part, part,
         )
-        near_parts.append(mine)
-        arrived.append(lax.ppermute(theirs, "shift", swap))
+        near_parts[one] = mine
+        arrived[one] = lax.ppermute(theirs, "shift", swap)
 
     total = downward(place, sigma, inc, interp_two, across, unfold, field, near_parts, shifts)
     total = join(place, total, arrived)

time: 162 us -> 160 us (0.988)
  waiting for transfers between devices: 48.4 us -> 7.01 us
  starting transfers between devices: 33.6 us -> 67.9 us
  local copies, waits for them, and re-layouts: 0.82 us -> 4.93 us
    ppermute x6 -> x9, waiting for transfers between devices: 34.8 us -> 0.02 us  [the longest x2 0.01 us: body(): lax.ppermute(lax.slice_in_dim(field, one * part, (one + 1) * part, axis=0...]
    all_to_all x1, starting transfers between devices: 6.97 us -> 41.6 us  [body(): lax.all_to_all(pieces, 'box', split_axis=0, concat_axis=0, tiled=True)]
    all_to_all x1, waiting for transfers between devices: 13.6 us -> 6.97 us  [body(): lax.all_to_all(pieces, 'box', split_axis=0, concat_axis=0, tiled=True)]
    all_to_all x1, starting transfers between devices: 6.77 us -> 4.26 us  [body(): lax.all_to_all(inc.reshape(count, grand, columns, chunk), 'box', split_ax...]
    unnamed x12 -> x16, local copies, waits for them, and re-layouts: 0.82 us -> 3.15 us
    ppermute x6 -> x9, starting transfers between devices: 14.2 us -> 16.4 us  [the longest x2 6.48 us: body(): pieces.append(lax.ppermute(swapped[one], 'box', up))]
    slice x0 -> x1, local copies, waits for them, and re-layouts: none -> 1.78 us  [body(): lax.slice_in_dim(field, one * part, (one + 1) * part, axis=0)]
  transfers between devices with their start and end apart: 10 -> 13, of which waited for: 2 -> 1; matrix products, arithmetic and copies ran while one was open for 0% -> 1% of each run, Pallas kernels for 45% -> 46%
where the time goes in v1:
time: 160 us; the launch traced here: 158 us
  Pallas kernels  77.3 us (48%)
  starting transfers between devices  67.9 us (42%)
  waiting for transfers between devices  7.01 us (4%)
  local copies, waits for them, and re-layouts  4.93 us (3%)
    all_to_all x1, starting transfers between devices, body(): lax.all_to_all(pieces, 'box', split_axis=0, concat_axis=0, tiled=True)  41.6 us
    pallas_call x2, Pallas kernels, near(): pl.pallas_call(functools.partial(near_kernel, first=first, count=count, c...  19 us
    pallas_call x1, Pallas kernels, downward(): pl.pallas_call(functools.partial(down_kernel, children=children, pair=pai...  15.2 us
    pallas_call x1, Pallas kernels, level1(): pl.pallas_call(level1_kernel, grid=(parents,), out_shape=(jax.ShapeDtypeS...  14.9 us
    pallas_call x1, Pallas kernels, coarsen(): pl.pallas_call(coarse_kernel, grid=(samples2 // rows, grand), out_shape=j...  11.4 us
    pallas_call x1, Pallas kernels, level2(): pl.pallas_call(level2_kernel, out_shape=jax.ShapeDtypeStruct((offset.shap...  7.11 us
    all_to_all x1, waiting for transfers between devices, body(): lax.all_to_all(pieces, 'box', split_axis=0, concat_axis=0, tiled=True)  6.97 us
    ppermute x2, starting transfers between devices, body(): pieces.append(lax.ppermute(swapped[one], 'box', up))  6.48 us
  transfers between devices with their start and end apart: 13, of which 1 were waited for; matrix products, arithmetic and copies ran while one was open for 1% of the time, Pallas kernels for 46%

profile of v1, /device:TPU:0, one launch (start us, length us, event | category | flops | bytes accessed | tf_op | source)
XLA Modules:
  0.0 157.8 jit_solution(6561749295488436147)
XLA Ops:
  0.0 1.3 collective-permute-start.1
  1.3 4.4 %collective-permute-start = (bf16[64,128,128]{2,1,0:T(8,128)(2,1)}, bf16[64,128,128]{2,1,0:T(8,128)(2,1)}, u32[]{:S(2)}, u32[]{:S(2)}) collective-permute-start(bf16[64,128,128]{2,1,0:T(8,128)(2,1)} %bitcast.22), channel_id=1, source_target_pairs={{0,2},{2,4},{4,6},{6,8},{8,10},{10,12},{12,14},{14,16},{16,18},{18... | collective-permute-start | bytes 6291464 | tf_op jit(solution)/shard_map/ppermute | solution.py:502
  5.7 1.8 %slice_bitcast_fusion = (bf16[32,128,128]{2,1,0:T(8,128)(2,1)S(1)}, bf16[32,128,128]{2,1,0:T(8,128)(2,1)S(1)}) fusion(bf16[1,64,128,128]{3,2,1,0:T(8,128)(2,1)} %param.13), kind=kLoop, calls=%fused_computation | loop fusion | bytes 4194304 | tf_op jit(solution)/shard_map/slice | solution.py:499
  7.4 3.1 %collective-permute-start.4 = (bf16[32,128,128]{2,1,0:T(8,128)(2,1)S(1)}, bf16[32,128,128]{2,1,0:T(8,128)(2,1)}, u32[]{:S(2)}, u32[]{:S(2)}) collective-permute-start(bf16[32,128,128]{2,1,0:T(8,128)(2,1)S(1)} %get-tuple-element.27), channel_id=1, source_target_pairs={{0,1},{1,0},{2,3},{3,2},{4,5},{5,4},{6,7},{7,6},{8,9},{9,8},{10,11... | collective-permute-start | bytes 3145736 | tf_op jit(solution)/shard_map/ppermute | solution.py:498
  10.6 5.4 %fold.1 = (bf16[512,1024]{1,0:T(8,128)(2,1)}, bf16[8,512,128]{2,1,0:T(8,128)(2,1)}, bf16[8,128,512]{2,1,0:T(8,128)(2,1)}) custom-call(bf16[8,512,128]{2,1,0:T(8,128)(2,1)} %one_ref.1, bf16[128,128]{1,0:T(8,128)(2,1)} %radiate_ref.1, bf16[8,1024,128]{2,1,0:T(8,128)(2,1)} %bitcast.23), custom_call_target="tpu_custom_call" | custom-call | flops 3000000000 | bytes 6291456 | tf_op jit(solution)/shard_map/fold/pallas_call | solution.py:57
  16.0 2.0 %collective-permute-start.2 = (bf16[64,128,128]{2,1,0:T(8,128)(2,1)}, bf16[64,128,128]{2,1,0:T(8,128)(2,1)}, u32[]{:S(2)}, u32[]{:S(2)}) collective-permute-start(bf16[64,128,128]{2,1,0:T(8,128)(2,1)} %collective-permute-done.1.high_ref), channel_id=1, source_target_pairs={{2,3},{3,2},{6,7},{7,6},{10,11},{11,10},{14,15},{15,14},{18,19},{1... | collective-permute-start | bytes 6291464 | tf_op jit(solution)/shard_map/ppermute | solution.py:531
  18.0 11.4 %coarsen.1 = bf16[1,2048,128]{2,1,0:T(8,128)(2,1)} custom-call(bf16[8,2048,512]{2,1,0:T(8,128)(2,1)} %two_ref.3, bf16[8,512,128]{2,1,0:T(8,128)(2,1)} %get-tuple-element.16.upper_ref), custom_call_target="tpu_custom_call" | custom-call | flops 4000000000 | bytes 18874368 | tf_op jit(solution)/shard_map/coarsen/pallas_call | solution.py:93
  29.4 41.6 %all-to-all-start = ((bf16[16,1,128,128]{3,2,1,0:T(8,128)(2,1)}), bf16[16,1,128,128]{3,2,1,0:T(8,128)(2,1)S(1)}, u32[]{:S(2)}, u32[]{:S(2)}) async-start(bf16[16,1,128,128]{3,2,1,0:T(8,128)(2,1)} %bitcast.28), calls=%async_computation | async-start | bytes 1048576 | tf_op jit(solution)/shard_map/all_to_all | solution.py:510
  71.0 1.3 collective-permute-start.8
  72.3 4.1 %collective-permute-start.6 = (bf16[32,128,128]{2,1,0:T(8,128)(2,1)}, bf16[32,128,128]{2,1,0:T(8,128)(2,1)S(1)}, u32[]{:S(2)}, u32[]{:S(2)}) collective-permute-start(bf16[32,128,128]{2,1,0:T(8,128)(2,1)} %collective-permute-done.4.rest_1_), channel_id=1, source_target_pairs={{0,2},{2,4},{4,6},{6,8},{8,10},{10,12},{12,14},{14,16},{16,18},{18... | collective-permute-start | bytes 3145736 | tf_op jit(solution)/shard_map/ppermute | solution.py:528
  76.4 1.3 collective-permute-start.7
  78.3 7.0 %all-to-all-done = bf16[16,1,128,128]{3,2,1,0:T(8,128)(2,1)S(1)} async-done(((bf16[16,1,128,128]{3,2,1,0:T(8,128)(2,1)}), bf16[16,1,128,128]{3,2,1,0:T(8,128)(2,1)S(1)}, u32[]{:S(2)}, u32[]{:S(2)}) %all-to-all-start) | async-done | bytes 524320 | tf_op jit(solution)/shard_map/all_to_all | solution.py:510
  85.3 7.1 %level2.1 = bf16[16,128,128]{2,1,0:T(8,128)(2,1)} custom-call(s32[16,32]{1,0:T(8,128)S(1)} %copy-done.2, s32[16,32]{1,0:T(8,128)S(1)} %copy-done.3, f32[316,128]{1,0:T(8,128)S(1)} %copy-done.1, bf16[16,128,128]{2,1,0:T(8,128)(2,1)S(1)} %bitcast.20), custom_call_target="tpu_custom_call" | custom-call | flops 3000000000 | bytes 2097152 | tf_op jit(solution)/shard_map/level2/pallas_call | solution.py:153
  92.4 4.3 %all-to-all-start.1 = ((bf16[16,1,128,128]{3,2,1,0:T(8,128)(2,1)}), bf16[16,1,128,128]{3,2,1,0:T(8,128)(2,1)S(1)}, u32[]{:S(2)}, u32[]{:S(2)}) async-start(bf16[16,1,128,128]{3,2,1,0:T(8,128)(2,1)} %bitcast.7), calls=%async_computation.1 | async-start | bytes 1048576 | tf_op jit(solution)/shard_map/all_to_all | solution.py:514
  96.7 2.4 %collective-permute-start.5 = (bf16[32,128,128]{2,1,0:T(8,128)(2,1)}, bf16[32,128,128]{2,1,0:T(8,128)(2,1)S(1)}, u32[]{:S(2)}, u32[]{:S(2)}) collective-permute-start(bf16[32,128,128]{2,1,0:T(8,128)(2,1)} %collective-permute-done.3.rest_0_), channel_id=1, source_target_pairs={{0,2},{2,4},{4,6},{6,8},{8,10},{10,12},{12,14},{14,16},{16,18},{18... | collective-permute-start | bytes 3145736 | tf_op jit(solution)/shard_map/ppermute | solution.py:528
  99.0 14.9 %level1.1 = (f32[8,128,512]{2,1,0:T(8,128)}, bf16[1024,512]{1,0:T(8,128)(2,1)}) custom-call(s32[2]{0:T(128)} %pad_add_fusion.place_ref, s32[8,16]{1,0:T(8,128)} %offset_ref.3, s32[8,16]{1,0:T(8,128)} %source_ref.3, f32[316,512]{1,0:T(8,128)} %table_ref.3, bf16[512,1024]{1,0:T(8,128)(2,1)} %get-tuple-element.17.fold_ref, ...), custom_call_target="tpu_custom_call" | custom-call | flops 8000000000 | bytes 14680064 | tf_op jit(solution)/shard_map/level1/pallas_call | solution.py:214
  114.0 0.9 copy-done.5
  115.3 9.5 %shard_map.128 = (f32[32,64,128]{2,1,0:T(8,128)}, bf16[32,64,128]{2,1,0:T(8,128)(2,1)}) custom-call(s32[2]{0:T(128)} %pad_add_fusion.place_ref, s32[6,64]{1,0:T(8,128)} %bitcast.29, bf16[64,6,64,128]{3,2,1,0:T(8,128)(2,1)} %blocks_ref.3, bf16[64,128,128]{2,1,0:T(8,128)(2,1)} %collective-permute-done.low_ref, bf16[64,128,128]{2,1,0:T(8,128)(2,1)} %bitcast.24, ...), custom_call_target="tpu_custom_call" | custom-call | flops 6400000000 | bytes 17880064 | tf_op jit(solution)/shard_map/pallas_call | solution.py:331
  125.3 1.0 copy-done.7
  126.3 9.5 %shard_map.127 = (f32[32,64,128]{2,1,0:T(8,128)}, bf16[32,64,128]{2,1,0:T(8,128)(2,1)}) custom-call(s32[2]{0:T(128)} %pad_add_fusion.place_ref, s32[6,64]{1,0:T(8,128)} %bitcast.30, bf16[64,6,64,128]{3,2,1,0:T(8,128)(2,1)} %blocks_ref.3, bf16[64,128,128]{2,1,0:T(8,128)(2,1)} %collective-permute-done.low_ref, bf16[64,128,128]{2,1,0:T(8,128)(2,1)} %bitcast.25, ...), custom_call_target="tpu_custom_call" | custom-call | flops 6400000000 | bytes 17880064 | tf_op jit(solution)/shard_map/pallas_call | solution.py:331
  135.8 1.6 %collective-permute-start.9 = (bf16[32,64,128]{2,1,0:T(8,128)(2,1)}, bf16[32,64,128]{2,1,0:T(8,128)(2,1)S(1)}, u32[]{:S(2)}, u32[]{:S(2)}) collective-permute-start(bf16[32,64,128]{2,1,0:T(8,128)(2,1)} %get-tuple-element.25), channel_id=1, source_target_pairs={{0,1},{1,0},{2,3},{3,2},{4,5},{5,4},{6,7},{7,6},{8,9},{9,8},{10,11... | collective-permute-start | bytes 1572872 | tf_op jit(solution)/shard_map/ppermute | solution.py:546
  137.4 0.9 copy-done.4
  138.3 15.2 %downward.1.total_ref = f32[64,128,128]{2,1,0:T(8,128)} custom-call(s32[2]{0:T(128)} %pad_add_fusion.place_ref, f32[1,2]{1,0:T(1,128)} %sigma_ref.1, bf16[1,16,128,128]{3,2,1,0:T(8,128)(2,1)} %bitcast.27, bf16[8,2048,512]{2,1,0:T(8,128)(2,1)} %two_ref.3, f32[8,128,512]{2,1,0:T(8,128)} %get-tuple-element.20.across_ref, ...), custom_call_target="tpu_custom_call" | custom-call | flops 6000000000 | bytes 31457280 | tf_op jit(solution)/shard_map/downward/pallas_call | solution.py:407
  153.5 4.4 %join.1 = f32[64,128,128]{2,1,0:T(8,128)} custom-call(s32[2]{0:T(128)S(1)} %copy-done, f32[64,128,128]{2,1,0:T(8,128)} %downward.1.total_ref, bf16[32,64,128]{2,1,0:T(8,128)(2,1)S(1)} %collective-permute-done.9.rest_0_, bf16[32,64,128]{2,1,0:T(8,128)(2,1)S(1)} %collective-permute-done.10.rest_1_), custom_call_target="tpu_custom_call", output_to_operand_aliasing={{}: (1, {})} | custom-call | flops 10000000 | bytes 5242880 | tf_op jit(solution)/shard_map/join/pallas_call | solution.py:452
  (28 shorter events, 1.6 us)
Async XLA Ops:
  0.0 16.0 %collective-permute-start.1 = (bf16[64,128,128]{2,1,0:T(8,128)(2,1)}, bf16[64,128,128]{2,1,0:T(8,128)(2,1)}, u32[]{:S(2)}, u32[]{:S(2)}) collective-permute-start(bf16[64,128,128]{2,1,0:T(8,128)(2,1)} %bitcast.21), channel_id=1, source_target_pairs={{2,0},{4,2},{6,4},{8,6},{10,8},{12,10},{14,12},{16,14},{18,16},{20... | collective-permute-start | bytes 6291464 | tf_op jit(solution)/shard_map/ppermute | solution.py:501
  1.3 95.4 %collective-permute-start = (bf16[64,128,128]{2,1,0:T(8,128)(2,1)}, bf16[64,128,128]{2,1,0:T(8,128)(2,1)}, u32[]{:S(2)}, u32[]{:S(2)}) collective-permute-start(bf16[64,128,128]{2,1,0:T(8,128)(2,1)} %bitcast.22), channel_id=1, source_target_pairs={{0,2},{2,4},{4,6},{6,8},{8,10},{10,12},{12,14},{14,16},{16,18},{18... | collective-permute-start | bytes 6291464 | tf_op jit(solution)/shard_map/ppermute | solution.py:502
  7.4 63.5 %collective-permute-start.4 = (bf16[32,128,128]{2,1,0:T(8,128)(2,1)S(1)}, bf16[32,128,128]{2,1,0:T(8,128)(2,1)}, u32[]{:S(2)}, u32[]{:S(2)}) collective-permute-start(bf16[32,128,128]{2,1,0:T(8,128)(2,1)S(1)} %get-tuple-element.27), channel_id=1, source_target_pairs={{0,1},{1,0},{2,3},{3,2},{4,5},{5,4},{6,7},{7,6},{8,9},{9,8},{10,11... | collective-permute-start | bytes 3145736 | tf_op jit(solution)/shard_map/ppermute | solution.py:498
  10.5 65.9 %collective-permute-start.3 = (bf16[32,128,128]{2,1,0:T(8,128)(2,1)S(1)}, bf16[32,128,128]{2,1,0:T(8,128)(2,1)}, u32[]{:S(2)}, u32[]{:S(2)}) collective-permute-start(bf16[32,128,128]{2,1,0:T(8,128)(2,1)S(1)} %get-tuple-element.28), channel_id=1, source_target_pairs={{0,1},{1,0},{2,3},{3,2},{4,5},{5,4},{6,7},{7,6},{8,9},{9,8},{10,11... | collective-permute-start | bytes 3145736 | tf_op jit(solution)/shard_map/ppermute | solution.py:498
  16.0 98.0 %collective-permute-start.2 = (bf16[64,128,128]{2,1,0:T(8,128)(2,1)}, bf16[64,128,128]{2,1,0:T(8,128)(2,1)}, u32[]{:S(2)}, u32[]{:S(2)}) collective-permute-start(bf16[64,128,128]{2,1,0:T(8,128)(2,1)} %collective-permute-done.1.high_ref), channel_id=1, source_target_pairs={{2,3},{3,2},{6,7},{7,6},{10,11},{11,10},{14,15},{15,14},{18,19},{1... | collective-permute-start | bytes 6291464 | tf_op jit(solution)/shard_map/ppermute | solution.py:531
  18.0 67.2 %copy-start.1 = (f32[316,128]{1,0:T(8,128)S(1)}, f32[316,128]{1,0:T(8,128)}, u32[]{:S(2)}) copy-start(f32[316,128]{1,0:T(8,128)} %table_ref.2) | copy-start | bytes 485380
  18.0 67.2 %copy-start.2 = (s32[16,32]{1,0:T(8,128)S(1)}, s32[16,32]{1,0:T(8,128)}, u32[]{:S(2)}) copy-start(s32[16,32]{1,0:T(8,128)} %offset_ref.2) | copy-start | bytes 6148
  18.0 67.2 %copy-start.3 = (s32[16,32]{1,0:T(8,128)S(1)}, s32[16,32]{1,0:T(8,128)}, u32[]{:S(2)}) copy-start(s32[16,32]{1,0:T(8,128)} %source_ref.2) | copy-start | bytes 6148
  29.4 55.8 %all-to-all-start = ((bf16[16,1,128,128]{3,2,1,0:T(8,128)(2,1)}), bf16[16,1,128,128]{3,2,1,0:T(8,128)(2,1)S(1)}, u32[]{:S(2)}, u32[]{:S(2)}) async-start(bf16[16,1,128,128]{3,2,1,0:T(8,128)(2,1)} %bitcast.28), calls=%async_computation | async-start | bytes 1048576 | tf_op jit(solution)/shard_map/all_to_all | solution.py:510
  71.0 42.9 %collective-permute-start.8 = (bf16[32,128,128]{2,1,0:T(8,128)(2,1)}, bf16[32,128,128]{2,1,0:T(8,128)(2,1)}, u32[]{:S(2)}, u32[]{:S(2)}) collective-permute-start(bf16[32,128,128]{2,1,0:T(8,128)(2,1)} %collective-permute-done.4.rest_1_), channel_id=1, source_target_pairs={{2,0},{6,4},{10,8},{14,12},{18,16},{22,20},{26,24},{30,28},{3,1},{... | collective-permute-start | bytes 3145736 | tf_op jit(solution)/shard_map/ppermute | solution.py:530
  72.3 41.6 %collective-permute-start.6 = (bf16[32,128,128]{2,1,0:T(8,128)(2,1)}, bf16[32,128,128]{2,1,0:T(8,128)(2,1)S(1)}, u32[]{:S(2)}, u32[]{:S(2)}) collective-permute-start(bf16[32,128,128]{2,1,0:T(8,128)(2,1)} %collective-permute-done.4.rest_1_), channel_id=1, source_target_pairs={{0,2},{2,4},{4,6},{6,8},{8,10},{10,12},{12,14},{14,16},{16,18},{18... | collective-permute-start | bytes 3145736 | tf_op jit(solution)/shard_map/ppermute | solution.py:528
  76.4 37.5 %collective-permute-start.7 = (bf16[32,128,128]{2,1,0:T(8,128)(2,1)}, bf16[32,128,128]{2,1,0:T(8,128)(2,1)S(1)}, u32[]{:S(2)}, u32[]{:S(2)}) collective-permute-start(bf16[32,128,128]{2,1,0:T(8,128)(2,1)} %collective-permute-done.3.rest_0_), channel_id=1, source_target_pairs={{2,0},{6,4},{10,8},{14,12},{18,16},{22,20},{26,24},{30,28},{3,1},{... | collective-permute-start | bytes 3145736 | tf_op jit(solution)/shard_map/ppermute | solution.py:530
  92.4 45.0 %all-to-all-start.1 = ((bf16[16,1,128,128]{3,2,1,0:T(8,128)(2,1)}), bf16[16,1,128,128]{3,2,1,0:T(8,128)(2,1)S(1)}, u32[]{:S(2)}, u32[]{:S(2)}) async-start(bf16[16,1,128,128]{3,2,1,0:T(8,128)(2,1)} %bitcast.7), calls=%async_computation.1 | async-start | bytes 1048576 | tf_op jit(solution)/shard_map/all_to_all | solution.py:514
  96.7 28.7 %collective-permute-start.5 = (bf16[32,128,128]{2,1,0:T(8,128)(2,1)}, bf16[32,128,128]{2,1,0:T(8,128)(2,1)S(1)}, u32[]{:S(2)}, u32[]{:S(2)}) collective-permute-start(bf16[32,128,128]{2,1,0:T(8,128)(2,1)} %collective-permute-done.3.rest_0_), channel_id=1, source_target_pairs={{0,2},{2,4},{4,6},{6,8},{8,10},{10,12},{12,14},{14,16},{16,18},{18... | collective-permute-start | bytes 3145736 | tf_op jit(solution)/shard_map/ppermute | solution.py:528
  113.9 1.0 copy-start.5
  113.9 1.3 copy-start.6
  124.8 28.7 %collective-permute-start.10 = (bf16[32,64,128]{2,1,0:T(8,128)(2,1)}, bf16[32,64,128]{2,1,0:T(8,128)(2,1)S(1)}, u32[]{:S(2)}, u32[]{:S(2)}) collective-permute-start(bf16[32,64,128]{2,1,0:T(8,128)(2,1)} %get-tuple-element.26), channel_id=1, source_target_pairs={{0,1},{1,0},{2,3},{3,2},{4,5},{5,4},{6,7},{7,6},{8,9},{9,8},{10,11... | collective-permute-start | bytes 1572872 | tf_op jit(solution)/shard_map/ppermute | solution.py:546
  125.3 1.0 copy-start.7
  135.8 17.6 %collective-permute-start.9 = (bf16[32,64,128]{2,1,0:T(8,128)(2,1)}, bf16[32,64,128]{2,1,0:T(8,128)(2,1)S(1)}, u32[]{:S(2)}, u32[]{:S(2)}) collective-permute-start(bf16[32,64,128]{2,1,0:T(8,128)(2,1)} %get-tuple-element.25), channel_id=1, source_target_pairs={{0,1},{1,0},{2,3},{3,2},{4,5},{5,4},{6,7},{7,6},{8,9},{9,8},{10,11... | collective-permute-start | bytes 1572872 | tf_op jit(solution)/shard_map/ppermute | solution.py:546
  137.4 0.9 copy-start.4
  138.3 15.2 %copy-start = (s32[2]{0:T(128)S(1)}, s32[2]{0:T(128)}, u32[]{:S(2)}) copy-start(s32[2]{0:T(128)} %pad_add_fusion.place_ref) | copy-start | bytes 28

commit v2 on v1

--- a/solution.py
+++ b/solution.py
@@ -112,7 +112,7 @@
     return total
 
 
-def list_sum(offset_ref, source_ref, box, shape, weight_at, pattern_at, base):
+def list_sum(offset_ref, source_ref, box, count, shape, weight_at, pattern_at, base):
     unroll = next(n for n in (4, 2, 1) if source_ref.shape[1] % n == 0)
 
     def add(trip, total):
@@ -124,7 +124,7 @@
             total = total + weight * pattern_at(jnp.where(live, named - base, 0))
         return total
 
-    trips = (live_count(source_ref, box) + unroll - 1) // unroll
+    trips = (count + unroll - 1) // unroll
     return lax.fori_loop(0, trips, add, jnp.zeros(shape, F32))
 
 
@@ -139,7 +139,7 @@
 
     def per_box(box, carry):
         total = list_sum(
-            offset_ref, source_ref, box, turned_ref.shape[1:],
+            offset_ref, source_ref, box, live_count(source_ref, box), turned_ref.shape[1:],
             lambda offset: table_ref[pl.ds(offset, 1), :], lambda source: turned_ref[source], 0,
         )
         out_ref[box] = total.astype(BF16)
@@ -169,36 +169,86 @@
     return jnp.einsum("cjk,cjkr->ckr", weights, picked, preferred_element_type=F32)
 
 
+def rise_kernel(fold_ref, turned_ref, high_ref, around_ref, unfold_ref):
+    pair, _, columns = high_ref.shape
+
+    @pl.when(pl.program_id(0) == 0)
+    def _():
+        for first in range(0, fold_ref.shape[1], 128):
+            unfold_ref[first : first + 128, :] = fold_ref[:, first : first + 128].T
+
+    wide = jnp.concatenate([high_ref[one] for one in range(pair)], axis=1)
+    pattern = jnp.dot(fold_ref[...], wide, preferred_element_type=F32)
+    for one in range(pair):
+        around_ref[0, one] = turned_ref[one].astype(F32)
+        around_ref[1, one] = pattern[:, one * columns : (one + 1) * columns].T.astype(BF16).astype(F32)
+
+
+def rise(folded, turned, high):
+    parents, columns, samples1 = turned.shape
+    width = high.shape[1]
+    pair = 2 if parents % 2 == 0 else 1
+    return pl.pallas_call(
+        rise_kernel,
+        grid=(parents // pair,),
+        out_shape=(
+            jax.ShapeDtypeStruct((2, parents, columns, samples1), F32),
+            jax.ShapeDtypeStruct((folded.shape[1], folded.shape[0]), BF16),
+        ),
+        in_specs=[
+            pl.BlockSpec(folded.shape, lambda i: (0, 0)),
+            pl.BlockSpec((pair, columns, samples1), lambda i: (i, 0, 0)),
+            pl.BlockSpec((pair, width, columns), lambda i: (i, 0, 0)),
+        ],
+        out_specs=(
+            pl.BlockSpec((2, pair, columns, samples1), lambda i: (0, i, 0, 0)),
+            pl.BlockSpec((folded.shape[1], folded.shape[0]), lambda i: (0, 0)),
+        ),
+        compiler_params=params(56),
+        cost_estimate=cost(2 * 10**9, 10 * 2**20),
+        name="rise",
+    )(folded, turned, high)
+
+
 def level1_kernel(
-    place_ref, offset_ref, source_ref, table_ref, fold_ref, turned_ref, low_ref, high_ref,
-    across_ref, unfold_ref, rim_ref, rows_ref,
+    place_ref, offset_ref, source_ref, table_ref, fold_ref, low_ref, around_ref,
+    across_ref, rim_ref, rows_ref, sem,
 ):
     step = pl.program_id(0)
-    parents, columns, samples1 = turned_ref.shape
+    pair, _, columns = low_ref.shape
+    parents, _, samples1 = across_ref.shape
     width = rows_ref.shape[2]
-    both = jnp.dot(
-        fold_ref[...],
-        jnp.concatenate([low_ref[0], high_ref[0]], axis=1),
-        preferred_element_type=F32,
-    )
-    rim_ref[step] = both[:, :columns].T.astype(BF16).astype(F32)
-    rim_ref[parents + step] = turned_ref[step].astype(F32)
-    rim_ref[2 * parents + step] = both[:, columns:].T.astype(BF16).astype(F32)
+
+    def around(which):
+        return pltpu.make_async_copy(
+            around_ref.at[which], rim_ref.at[pl.ds((which + 1) * parents, parents)], sem.at[which]
+        )
 
     @pl.when(step == 0)
     def _():
+        around(0).start()
+        around(1).start()
         for part in range(rows_ref.shape[0]):
             rows_ref[part] = table_ref[:, part * width : (part + 1) * width]
-        for first in range(0, fold_ref.shape[1], 128):
-            unfold_ref[first : first + 128, :] = fold_ref[:, first : first + 128].T
-
-    @pl.when(step == parents - 1)
+
+    wide = jnp.concatenate([low_ref[one] for one in range(pair)], axis=1)
+    pattern = jnp.dot(fold_ref[...], wide, preferred_element_type=F32)
+    for one in range(pair):
+        rim_ref[step * pair + one] = (
+            pattern[:, one * columns : (one + 1) * columns].T.astype(BF16).astype(F32)
+        )
+
+    @pl.when(step == pl.num_programs(0) - 1)
     def _():
+        around(0).wait()
+        around(1).wait()
+
         def per_box(box, carry):
+            count = live_count(source_ref, box)
             for part in range(samples1 // width):
                 lanes = slice(part * width, (part + 1) * width)
                 across_ref[box, :, lanes] = list_sum(
-                    offset_ref, source_ref, box, (columns, width),
+                    offset_ref, source_ref, box, count, (columns, width),
                     lambda offset: rows_ref[part, pl.ds(offset, 1), :],
                     lambda source: rim_ref[source, :, lanes],
                     place_ref[0] * parents - parents,
@@ -208,36 +258,30 @@
         lax.fori_loop(0, parents, per_box, 0)
 
 
-def level1(place, offset, source, table, folded, turned, low, high):
-    parents, columns, samples1 = turned.shape
-    around = pl.BlockSpec((1,) + low.shape[1:], lambda i: (i, 0, 0))
+def level1(place, offset, source, table, folded, low, around):
+    _, parents, columns, samples1 = around.shape
+    pair = 2 if parents % 2 == 0 else 1
     return pl.pallas_call(
         level1_kernel,
-        grid=(parents,),
-        out_shape=(
-            jax.ShapeDtypeStruct((parents, columns, samples1), F32),
-            jax.ShapeDtypeStruct((folded.shape[1], folded.shape[0]), BF16),
-        ),
+        grid=(parents // pair,),
+        out_shape=jax.ShapeDtypeStruct((parents, columns, samples1), F32),
         in_specs=[smem()] * 3
         + [
             pl.BlockSpec(table.shape, lambda i: (0, 0)),
             pl.BlockSpec(folded.shape, lambda i: (0, 0)),
-            pl.BlockSpec(turned.shape, lambda i: (0, 0, 0)),
-            around,
-            around,
-        ],
-        out_specs=(
-            pl.BlockSpec((parents, columns, samples1), lambda i: (0, 0, 0)),
-            pl.BlockSpec((folded.shape[1], folded.shape[0]), lambda i: (0, 0)),
-        ),
+            pl.BlockSpec((pair,) + low.shape[1:], lambda i: (i, 0, 0)),
+            pl.BlockSpec(memory_space=pl.ANY),
+        ],
+        out_specs=pl.BlockSpec((parents, columns, samples1), lambda i: (0, 0, 0)),
         scratch_shapes=[
             pltpu.VMEM((3 * parents, columns, samples1), F32),
             pltpu.VMEM((samples1 // 128, table.shape[0], 128), F32),
+            pltpu.SemaphoreType.DMA((2,)),
         ],
         compiler_params=params(56),
-        cost_estimate=cost(8 * 10**9, 14 * 2**20),
+        cost_estimate=cost(6 * 10**9, 12 * 2**20),
         name="level1",
-    )(place, offset, source, table, folded, turned, low, high)
+    )(place, offset, source, table, folded, low, around)
 
 
 def near_kernel(
@@ -359,7 +403,7 @@
 
 
 def down_kernel(place_ref, sigma_ref, inc_ref, two_ref, across_ref, unfold_ref, field_ref, *rest, children, pair, parts, shifts):
-    near_refs, (out_ref, flat_ref, local_ref) = rest[:parts], rest[parts:]
+    near_refs, early_ref, (out_ref, flat_ref, local_ref) = rest[:parts], rest[parts], rest[parts + 1 :]
     chunks, columns, lanes = inc_ref.shape[1:]
     step = pl.program_id(0)
     span_of = pl.num_programs(0) // parts
@@ -394,8 +438,13 @@
                 def _():
                     out_ref[:, shift * rows : (shift + 1) * rows, :] += near_ref[...]
 
-
-def downward(place, sigma, inc, interp_two, across, unfold, field, near_parts, shifts):
+            @pl.when((place_ref[1] == shift) & (step // span_of == parts - 1))
+            def _():
+                there = shifts - 1 - shift
+                out_ref[:, there * rows : (there + 1) * rows, :] += early_ref[...].astype(F32)
+
+
+def downward(place, sigma, inc, interp_two, across, unfold, field, near_parts, early, shifts):
     grand, chunks, columns, lanes = inc.shape
     children, samples2, samples1 = interp_two.shape
     boxes, unknowns, _ = field.shape
@@ -419,7 +468,7 @@
         ]
         + [
             pl.BlockSpec((per, rows, columns), lambda c, part=part: part_index(part, each)(c // pair))
-            for part in range(parts)
+            for part in list(range(parts)) + [parts - 1]
         ],
         out_specs=pl.BlockSpec((per, unknowns, columns), lambda c: (c // pair, 0, 0)),
         scratch_shapes=[
@@ -429,44 +478,31 @@
         compiler_params=params(56),
         cost_estimate=cost(6 * 10**9, 30 * 2**20),
         name="downward",
-    )(place, sigma, inc, interp_two, across, unfold, field, *near_parts)
-
-
-def join_kernel(place_ref, total_ref, *rest, parts):
-    part_refs, out_ref = rest[:parts], rest[parts]
-    each = pl.num_programs(0) // parts
-    for part, part_ref in enumerate(part_refs):
-
-        @pl.when(pl.program_id(0) // each == part)
-        def _():
-            out_ref[...] = total_ref[...] + part_ref[...].astype(F32)
-
-
-def join(place, total, arrived):
-    boxes, _, columns = total.shape
-    count, rows, _ = arrived[0].shape
-    parts = len(arrived)
+    )(place, sigma, inc, interp_two, across, unfold, field, *near_parts, early)
+
+
+def join_kernel(place_ref, total_ref, part_ref, out_ref):
+    out_ref[...] = total_ref[...] + part_ref[...].astype(F32)
+
+
+def join(place, total, part):
+    count, rows, columns = part.shape
     step = min(16, count)
-    each = count // step
     half = pl.BlockSpec((step, rows, columns), lambda i, place_ref: (i, 1 - place_ref[1], 0))
     return pl.pallas_call(
-        functools.partial(join_kernel, parts=parts),
+        join_kernel,
         grid_spec=pltpu.PrefetchScalarGridSpec(
             num_scalar_prefetch=1,
-            grid=(boxes // step,),
-            in_specs=[half]
-            + [
-                pl.BlockSpec((step, rows, columns), lambda i, place_ref, part=part: part_index(part, each)(i))
-                for part in range(parts)
-            ],
+            grid=(count // step,),
+            in_specs=[half, pl.BlockSpec((step, rows, columns), lambda i, place_ref: (i, 0, 0))],
             out_specs=half,
         ),
         out_shape=jax.ShapeDtypeStruct(total.shape, F32),
         input_output_aliases={1: 0},
         compiler_params=params(10),
-        cost_estimate=cost(10**7, 5 * 2**20),
+        cost_estimate=cost(10**7, 3 * 2**20),
         name="join",
-    )(place, total, *arrived)
+    )(place, total, part)
 
 
 def body(
@@ -531,9 +567,9 @@
     high_odd = lax.ppermute(high, ("box", "shift"), odd_swap)
 
     wide = (parents, children * unknowns, columns)
-    across, unfold = level1(
-        place, level1_offset, level1_source, trans_one, folded, turned,
-        low.reshape(wide), high.reshape(wide),
+    around, unfold = rise(folded, turned, high.reshape(wide))
+    across = level1(
+        place, level1_offset, level1_source, trans_one, folded, low.reshape(wide), around
     )
     low, across = lax.optimization_barrier((low, across))
     near_parts, arrived = [None] * splits, [None] * splits
@@ -545,8 +581,10 @@
         near_parts[one] = mine
         arrived[one] = lax.ppermute(theirs, "shift", swap)
 
-    total = downward(place, sigma, inc, interp_two, across, unfold, field, near_parts, shifts)
-    total = join(place, total, arrived)
+    total = downward(
+        place, sigma, inc, interp_two, across, unfold, field, near_parts, arrived[-1], shifts
+    )
+    total = join(place, total, arrived[0])
     return total[None]
 
 

time: 160 us -> 162 us (1.012)
  waiting for transfers between devices: 7.01 us -> 9.62 us
  starting transfers between devices: 67.9 us -> 66.1 us
    ppermute x2, starting transfers between devices: 6.48 us -> 4.74 us  [body(): pieces.append(lax.ppermute(swapped[one], 'box', up))]
    all_to_all x1, waiting for transfers between devices: 6.97 us -> 8.6 us  [body(): lax.all_to_all(pieces, 'box', split_axis=0, concat_axis=0, tiled=True)]
    pallas_call x2 -> x3, Pallas kernels: 19.2 us -> 19.8 us  [the longest x1 10.7 us: level1(): pl.pallas_call(level1_kernel, grid=(parents // pair,), out_shape=jax.Shap...]
  transfers between devices with their start and end apart: 13 -> 13, of which waited for: 1 -> 2; matrix products, arithmetic and copies ran while one was open for 1% -> 2% of each run, Pallas kernels for 46% -> 47%
where the time goes in v2:
time: 162 us; the launch traced here: 160 us
  Pallas kernels  78.1 us (48%)
  starting transfers between devices  66.1 us (41%)
  waiting for transfers between devices  9.62 us (6%)
  local copies, waits for them, and re-layouts  4.84 us (3%)
    all_to_all x1, starting transfers between devices, body(): lax.all_to_all(pieces, 'box', split_axis=0, concat_axis=0, tiled=True)  41.6 us
    pallas_call x2, Pallas kernels, near(): pl.pallas_call(functools.partial(near_kernel, first=first, count=count, c...  19 us
    pallas_call x1, Pallas kernels, downward(): pl.pallas_call(functools.partial(down_kernel, children=children, pair=pai...  15.4 us
    pallas_call x1, Pallas kernels, coarsen(): pl.pallas_call(coarse_kernel, grid=(samples2 // rows, grand), out_shape=j...  11.4 us
    pallas_call x1, Pallas kernels, level1(): pl.pallas_call(level1_kernel, grid=(parents // pair,), out_shape=jax.Shap...  10.7 us
    all_to_all x1, waiting for transfers between devices, body(): lax.all_to_all(pieces, 'box', split_axis=0, concat_axis=0, tiled=True)  8.6 us
    pallas_call x1, Pallas kernels, level2(): pl.pallas_call(level2_kernel, out_shape=jax.ShapeDtypeStruct((offset.shap...  7.13 us
    pallas_call x1, Pallas kernels, rise(): pl.pallas_call(rise_kernel, grid=(parents // pair,), out_shape=(jax.Shape...  6.43 us
  transfers between devices with their start and end apart: 13, of which 2 were waited for; matrix products, arithmetic and copies ran while one was open for 2% of the time, Pallas kernels for 47%

profile of v2, /device:TPU:0, one launch (start us, length us, event | category | flops | bytes accessed | tf_op | source)
XLA Modules:
  0.0 159.5 jit_solution(1461465920201581161)
XLA Ops:
  0.0 1.3 collective-permute-start.1
  1.3 4.4 %collective-permute-start = (bf16[64,128,128]{2,1,0:T(8,128)(2,1)}, bf16[64,128,128]{2,1,0:T(8,128)(2,1)}, u32[]{:S(2)}, u32[]{:S(2)}) collective-permute-start(bf16[64,128,128]{2,1,0:T(8,128)(2,1)} %bitcast.22), channel_id=1, source_target_pairs={{0,2},{2,4},{4,6},{6,8},{8,10},{10,12},{12,14},{14,16},{16,18},{18... | collective-permute-start | bytes 6291464 | tf_op jit(solution)/shard_map/ppermute | solution.py:538
  5.7 1.8 %slice_bitcast_fusion = (bf16[32,128,128]{2,1,0:T(8,128)(2,1)S(1)}, bf16[32,128,128]{2,1,0:T(8,128)(2,1)S(1)}) fusion(bf16[1,64,128,128]{3,2,1,0:T(8,128)(2,1)} %param.13), kind=kLoop, calls=%fused_computation | loop fusion | bytes 4194304 | tf_op jit(solution)/shard_map/slice | solution.py:535
  7.5 3.1 %collective-permute-start.3 = (bf16[32,128,128]{2,1,0:T(8,128)(2,1)S(1)}, bf16[32,128,128]{2,1,0:T(8,128)(2,1)}, u32[]{:S(2)}, u32[]{:S(2)}) collective-permute-start(bf16[32,128,128]{2,1,0:T(8,128)(2,1)S(1)} %get-tuple-element.28), channel_id=1, source_target_pairs={{0,1},{1,0},{2,3},{3,2},{4,5},{5,4},{6,7},{7,6},{8,9},{9,8},{10,11... | collective-permute-start | bytes 3145736 | tf_op jit(solution)/shard_map/ppermute | solution.py:534
  10.6 5.4 %fold.1 = (bf16[512,1024]{1,0:T(8,128)(2,1)}, bf16[8,512,128]{2,1,0:T(8,128)(2,1)}, bf16[8,128,512]{2,1,0:T(8,128)(2,1)}) custom-call(bf16[8,512,128]{2,1,0:T(8,128)(2,1)} %one_ref.1, bf16[128,128]{1,0:T(8,128)(2,1)} %radiate_ref.1, bf16[8,1024,128]{2,1,0:T(8,128)(2,1)} %bitcast.23), custom_call_target="tpu_custom_call" | custom-call | flops 3000000000 | bytes 6291456 | tf_op jit(solution)/shard_map/fold/pallas_call | solution.py:57
  16.0 2.0 %collective-permute-start.2 = (bf16[64,128,128]{2,1,0:T(8,128)(2,1)}, bf16[64,128,128]{2,1,0:T(8,128)(2,1)}, u32[]{:S(2)}, u32[]{:S(2)}) collective-permute-start(bf16[64,128,128]{2,1,0:T(8,128)(2,1)} %collective-permute-done.1.high_ref), channel_id=1, source_target_pairs={{2,3},{3,2},{6,7},{7,6},{10,11},{11,10},{14,15},{15,14},{18,19},{1... | collective-permute-start | bytes 6291464 | tf_op jit(solution)/shard_map/ppermute | solution.py:567
  18.0 11.4 %coarsen.1 = bf16[1,2048,128]{2,1,0:T(8,128)(2,1)} custom-call(bf16[8,2048,512]{2,1,0:T(8,128)(2,1)} %two_ref.3, bf16[8,512,128]{2,1,0:T(8,128)(2,1)} %get-tuple-element.16.upper_ref), custom_call_target="tpu_custom_call" | custom-call | flops 4000000000 | bytes 18874368 | tf_op jit(solution)/shard_map/coarsen/pallas_call | solution.py:93
  29.4 41.6 %all-to-all-start = ((bf16[16,1,128,128]{3,2,1,0:T(8,128)(2,1)}), bf16[16,1,128,128]{3,2,1,0:T(8,128)(2,1)S(1)}, u32[]{:S(2)}, u32[]{:S(2)}) async-start(bf16[16,1,128,128]{3,2,1,0:T(8,128)(2,1)} %bitcast.28), calls=%async_computation | async-start | bytes 1048576 | tf_op jit(solution)/shard_map/all_to_all | solution.py:546
  71.0 2.4 %collective-permute-start.6 = (bf16[32,128,128]{2,1,0:T(8,128)(2,1)}, bf16[32,128,128]{2,1,0:T(8,128)(2,1)S(1)}, u32[]{:S(2)}, u32[]{:S(2)}) collective-permute-start(bf16[32,128,128]{2,1,0:T(8,128)(2,1)} %collective-permute-done.4.rest_1_), channel_id=1, source_target_pairs={{0,2},{2,4},{4,6},{6,8},{8,10},{10,12},{12,14},{14,16},{16,18},{18... | collective-permute-start | bytes 3145736 | tf_op jit(solution)/shard_map/ppermute | solution.py:564
  73.4 1.3 collective-permute-start.8
  74.7 1.3 collective-permute-start.7
  76.7 8.6 %all-to-all-done = bf16[16,1,128,128]{3,2,1,0:T(8,128)(2,1)S(1)} async-done(((bf16[16,1,128,128]{3,2,1,0:T(8,128)(2,1)}), bf16[16,1,128,128]{3,2,1,0:T(8,128)(2,1)S(1)}, u32[]{:S(2)}, u32[]{:S(2)}) %all-to-all-start) | async-done | bytes 524320 | tf_op jit(solution)/shard_map/all_to_all | solution.py:546
  85.3 7.1 %level2.1 = bf16[16,128,128]{2,1,0:T(8,128)(2,1)} custom-call(s32[16,32]{1,0:T(8,128)S(1)} %copy-done.2, s32[16,32]{1,0:T(8,128)S(1)} %copy-done.3, f32[316,128]{1,0:T(8,128)S(1)} %copy-done.1, bf16[16,128,128]{2,1,0:T(8,128)(2,1)S(1)} %bitcast.20), custom_call_target="tpu_custom_call" | custom-call | flops 3000000000 | bytes 2097152 | tf_op jit(solution)/shard_map/level2/pallas_call | solution.py:153
  92.4 4.3 %all-to-all-start.1 = ((bf16[16,1,128,128]{3,2,1,0:T(8,128)(2,1)}), bf16[16,1,128,128]{3,2,1,0:T(8,128)(2,1)S(1)}, u32[]{:S(2)}, u32[]{:S(2)}) async-start(bf16[16,1,128,128]{3,2,1,0:T(8,128)(2,1)} %bitcast.7), calls=%async_computation.1 | async-start | bytes 1048576 | tf_op jit(solution)/shard_map/all_to_all | solution.py:550
  96.7 6.4 %rise.1 = (f32[2,8,128,512]{3,2,1,0:T(8,128)}, bf16[1024,512]{1,0:T(8,128)(2,1)}) custom-call(bf16[512,1024]{1,0:T(8,128)(2,1)} %get-tuple-element.17.fold_ref, bf16[8,128,512]{2,1,0:T(8,128)(2,1)} %get-tuple-element.18.turned_ref, bf16[8,1024,128]{2,1,0:T(8,128)(2,1)} %bitcast.11.high_ref), custom_call_target="tpu_custom_call" | custom-call | flops 2000000000 | bytes 10485760 | tf_op jit(solution)/shard_map/rise/pallas_call | solution.py:191
  103.1 2.4 %collective-permute-start.5 = (bf16[32,128,128]{2,1,0:T(8,128)(2,1)}, bf16[32,128,128]{2,1,0:T(8,128)(2,1)S(1)}, u32[]{:S(2)}, u32[]{:S(2)}) collective-permute-start(bf16[32,128,128]{2,1,0:T(8,128)(2,1)} %collective-permute-done.3.rest_0_), channel_id=1, source_target_pairs={{0,2},{2,4},{4,6},{6,8},{8,10},{10,12},{12,14},{14,16},{16,18},{18... | collective-permute-start | bytes 3145736 | tf_op jit(solution)/shard_map/ppermute | solution.py:564
  105.5 10.7 %level1.1.across_ref = f32[8,128,512]{2,1,0:T(8,128)} custom-call(s32[2]{0:T(128)} %pad_add_fusion.place_ref, s32[8,16]{1,0:T(8,128)} %offset_ref.3, s32[8,16]{1,0:T(8,128)} %source_ref.3, f32[316,512]{1,0:T(8,128)} %table_ref.3, bf16[512,1024]{1,0:T(8,128)(2,1)} %get-tuple-element.17.fold_ref, bf16[8,1024,128]{2,1,0:T(8,128)(2,1)} %bitcast.10.low_ref, ...), custom_call_target="tpu_custom_call" | custom-call | flops 6000000000 | bytes 12582912 | tf_op jit(solution)/shard_map/level1/pallas_call | solution.py:264
  117.6 9.5 %shard_map.128 = (f32[32,64,128]{2,1,0:T(8,128)}, bf16[32,64,128]{2,1,0:T(8,128)(2,1)}) custom-call(s32[2]{0:T(128)} %pad_add_fusion.place_ref, s32[6,64]{1,0:T(8,128)} %bitcast.29, bf16[64,6,64,128]{3,2,1,0:T(8,128)(2,1)} %blocks_ref.3, bf16[64,128,128]{2,1,0:T(8,128)(2,1)} %collective-permute-done.low_ref, bf16[64,128,128]{2,1,0:T(8,128)(2,1)} %bitcast.24, ...), custom_call_target="tpu_custom_call" | custom-call | flops 6400000000 | bytes 17880064 | tf_op jit(solution)/shard_map/pallas_call | solution.py:375
  127.7 1.0 copy-done.8
  128.7 9.5 %shard_map.127 = (f32[32,64,128]{2,1,0:T(8,128)}, bf16[32,64,128]{2,1,0:T(8,128)(2,1)}) custom-call(s32[2]{0:T(128)} %pad_add_fusion.place_ref, s32[6,64]{1,0:T(8,128)} %bitcast.30, bf16[64,6,64,128]{3,2,1,0:T(8,128)(2,1)} %blocks_ref.3, bf16[64,128,128]{2,1,0:T(8,128)(2,1)} %collective-permute-done.low_ref, bf16[64,128,128]{2,1,0:T(8,128)(2,1)} %bitcast.25, ...), custom_call_target="tpu_custom_call" | custom-call | flops 6400000000 | bytes 17880064 | tf_op jit(solution)/shard_map/pallas_call | solution.py:375
  138.2 1.6 collective-permute-start.10
  139.7 1.0 collective-permute-done.9.rest_2_
  141.5 15.4 %downward.1.total_ref = f32[64,128,128]{2,1,0:T(8,128)} custom-call(s32[2]{0:T(128)} %pad_add_fusion.place_ref, f32[1,2]{1,0:T(1,128)} %sigma_ref.1, bf16[1,16,128,128]{3,2,1,0:T(8,128)(2,1)} %bitcast.27, bf16[8,2048,512]{2,1,0:T(8,128)(2,1)} %two_ref.3, f32[8,128,512]{2,1,0:T(8,128)} %level1.1.across_ref, bf16[1024,512]{1,0:T(8,128)(2,1)} %get-tuple-element.21.unfold_ref, ...), custom_call_target="tpu_custom_call" | custom-call | flops 6000000000 | bytes 31457280 | tf_op jit(solution)/shard_map/downward/pallas_call | solution.py:456
  156.9 2.6 %join.1 = f32[64,128,128]{2,1,0:T(8,128)} custom-call(s32[2]{0:T(128)S(1)} %copy-done, f32[64,128,128]{2,1,0:T(8,128)} %downward.1.total_ref, bf16[32,64,128]{2,1,0:T(8,128)(2,1)S(1)} %collective-permute-done.10.part_ref), custom_call_target="tpu_custom_call", output_to_operand_aliasing={{}: (1, {})} | custom-call | flops 10000000 | bytes 3145728 | tf_op jit(solution)/shard_map/join/pallas_call | solution.py:492
  (31 shorter events, 3.4 us)
Async XLA Ops:
  0.0 16.0 %collective-permute-start.1 = (bf16[64,128,128]{2,1,0:T(8,128)(2,1)}, bf16[64,128,128]{2,1,0:T(8,128)(2,1)}, u32[]{:S(2)}, u32[]{:S(2)}) collective-permute-start(bf16[64,128,128]{2,1,0:T(8,128)(2,1)} %bitcast.21), channel_id=1, source_target_pairs={{2,0},{4,2},{6,4},{8,6},{10,8},{12,10},{14,12},{16,14},{18,16},{20... | collective-permute-start | bytes 6291464 | tf_op jit(solution)/shard_map/ppermute | solution.py:537
  1.3 101.8 %collective-permute-start = (bf16[64,128,128]{2,1,0:T(8,128)(2,1)}, bf16[64,128,128]{2,1,0:T(8,128)(2,1)}, u32[]{:S(2)}, u32[]{:S(2)}) collective-permute-start(bf16[64,128,128]{2,1,0:T(8,128)(2,1)} %bitcast.22), channel_id=1, source_target_pairs={{0,2},{2,4},{4,6},{6,8},{8,10},{10,12},{12,14},{14,16},{16,18},{18... | collective-permute-start | bytes 6291464 | tf_op jit(solution)/shard_map/ppermute | solution.py:538
  7.5 67.2 %collective-permute-start.3 = (bf16[32,128,128]{2,1,0:T(8,128)(2,1)S(1)}, bf16[32,128,128]{2,1,0:T(8,128)(2,1)}, u32[]{:S(2)}, u32[]{:S(2)}) collective-permute-start(bf16[32,128,128]{2,1,0:T(8,128)(2,1)S(1)} %get-tuple-element.28), channel_id=1, source_target_pairs={{0,1},{1,0},{2,3},{3,2},{4,5},{5,4},{6,7},{7,6},{8,9},{9,8},{10,11... | collective-permute-start | bytes 3145736 | tf_op jit(solution)/shard_map/ppermute | solution.py:534
  10.5 60.5 %collective-permute-start.4 = (bf16[32,128,128]{2,1,0:T(8,128)(2,1)S(1)}, bf16[32,128,128]{2,1,0:T(8,128)(2,1)}, u32[]{:S(2)}, u32[]{:S(2)}) collective-permute-start(bf16[32,128,128]{2,1,0:T(8,128)(2,1)S(1)} %get-tuple-element.27), channel_id=1, source_target_pairs={{0,1},{1,0},{2,3},{3,2},{4,5},{5,4},{6,7},{7,6},{8,9},{9,8},{10,11... | collective-permute-start | bytes 3145736 | tf_op jit(solution)/shard_map/ppermute | solution.py:534
  16.0 100.3 %collective-permute-start.2 = (bf16[64,128,128]{2,1,0:T(8,128)(2,1)}, bf16[64,128,128]{2,1,0:T(8,128)(2,1)}, u32[]{:S(2)}, u32[]{:S(2)}) collective-permute-start(bf16[64,128,128]{2,1,0:T(8,128)(2,1)} %collective-permute-done.1.high_ref), channel_id=1, source_target_pairs={{2,3},{3,2},{6,7},{7,6},{10,11},{11,10},{14,15},{15,14},{18,19},{1... | collective-permute-start | bytes 6291464 | tf_op jit(solution)/shard_map/ppermute | solution.py:567
  18.0 67.3 %copy-start.1 = (f32[316,128]{1,0:T(8,128)S(1)}, f32[316,128]{1,0:T(8,128)}, u32[]{:S(2)}) copy-start(f32[316,128]{1,0:T(8,128)} %table_ref.2) | copy-start | bytes 485380
  18.0 67.3 %copy-start.2 = (s32[16,32]{1,0:T(8,128)S(1)}, s32[16,32]{1,0:T(8,128)}, u32[]{:S(2)}) copy-start(s32[16,32]{1,0:T(8,128)} %offset_ref.2) | copy-start | bytes 6148
  18.0 67.3 %copy-start.3 = (s32[16,32]{1,0:T(8,128)S(1)}, s32[16,32]{1,0:T(8,128)}, u32[]{:S(2)}) copy-start(s32[16,32]{1,0:T(8,128)} %source_ref.2) | copy-start | bytes 6148
  29.4 55.9 %all-to-all-start = ((bf16[16,1,128,128]{3,2,1,0:T(8,128)(2,1)}), bf16[16,1,128,128]{3,2,1,0:T(8,128)(2,1)S(1)}, u32[]{:S(2)}, u32[]{:S(2)}) async-start(bf16[16,1,128,128]{3,2,1,0:T(8,128)(2,1)} %bitcast.28), calls=%async_computation | async-start | bytes 1048576 | tf_op jit(solution)/shard_map/all_to_all | solution.py:546
  71.0 45.2 %collective-permute-start.6 = (bf16[32,128,128]{2,1,0:T(8,128)(2,1)}, bf16[32,128,128]{2,1,0:T(8,128)(2,1)S(1)}, u32[]{:S(2)}, u32[]{:S(2)}) collective-permute-start(bf16[32,128,128]{2,1,0:T(8,128)(2,1)} %collective-permute-done.4.rest_1_), channel_id=1, source_target_pairs={{0,2},{2,4},{4,6},{6,8},{8,10},{10,12},{12,14},{14,16},{16,18},{18... | collective-permute-start | bytes 3145736 | tf_op jit(solution)/shard_map/ppermute | solution.py:564
  73.4 42.9 %collective-permute-start.8 = (bf16[32,128,128]{2,1,0:T(8,128)(2,1)}, bf16[32,128,128]{2,1,0:T(8,128)(2,1)}, u32[]{:S(2)}, u32[]{:S(2)}) collective-permute-start(bf16[32,128,128]{2,1,0:T(8,128)(2,1)} %collective-permute-done.4.rest_1_), channel_id=1, source_target_pairs={{2,0},{6,4},{10,8},{14,12},{18,16},{22,20},{26,24},{30,28},{3,1},{... | collective-permute-start | bytes 3145736 | tf_op jit(solution)/shard_map/ppermute | solution.py:566
  74.7 41.6 %collective-permute-start.7 = (bf16[32,128,128]{2,1,0:T(8,128)(2,1)}, bf16[32,128,128]{2,1,0:T(8,128)(2,1)S(1)}, u32[]{:S(2)}, u32[]{:S(2)}) collective-permute-start(bf16[32,128,128]{2,1,0:T(8,128)(2,1)} %collective-permute-done.3.rest_0_), channel_id=1, source_target_pairs={{2,0},{6,4},{10,8},{14,12},{18,16},{22,20},{26,24},{30,28},{3,1},{... | collective-permute-start | bytes 3145736 | tf_op jit(solution)/shard_map/ppermute | solution.py:566
  92.4 47.3 %all-to-all-start.1 = ((bf16[16,1,128,128]{3,2,1,0:T(8,128)(2,1)}), bf16[16,1,128,128]{3,2,1,0:T(8,128)(2,1)S(1)}, u32[]{:S(2)}, u32[]{:S(2)}) async-start(bf16[16,1,128,128]{3,2,1,0:T(8,128)(2,1)} %bitcast.7), calls=%async_computation.1 | async-start | bytes 1048576 | tf_op jit(solution)/shard_map/all_to_all | solution.py:550
  103.1 24.5 %collective-permute-start.5 = (bf16[32,128,128]{2,1,0:T(8,128)(2,1)}, bf16[32,128,128]{2,1,0:T(8,128)(2,1)S(1)}, u32[]{:S(2)}, u32[]{:S(2)}) collective-permute-start(bf16[32,128,128]{2,1,0:T(8,128)(2,1)} %collective-permute-done.3.rest_0_), channel_id=1, source_target_pairs={{0,2},{2,4},{4,6},{6,8},{8,10},{10,12},{12,14},{14,16},{16,18},{18... | collective-permute-start | bytes 3145736 | tf_op jit(solution)/shard_map/ppermute | solution.py:564
  116.3 1.0 copy-start.6
  116.3 1.3 copy-start.7
  127.1 13.6 %collective-permute-start.9 = (bf16[32,64,128]{2,1,0:T(8,128)(2,1)}, bf16[32,64,128]{2,1,0:T(8,128)(2,1)S(1)}, u32[]{:S(2)}, u32[]{:S(2)}) collective-permute-start(bf16[32,64,128]{2,1,0:T(8,128)(2,1)} %get-tuple-element.25), channel_id=1, source_target_pairs={{0,1},{1,0},{2,3},{3,2},{4,5},{5,4},{6,7},{7,6},{8,9},{9,8},{10,11... | collective-permute-start | bytes 1572872 | tf_op jit(solution)/shard_map/ppermute | solution.py:582
  127.7 1.0 copy-start.8
  138.2 18.8 %collective-permute-start.10 = (bf16[32,64,128]{2,1,0:T(8,128)(2,1)}, bf16[32,64,128]{2,1,0:T(8,128)(2,1)S(1)}, u32[]{:S(2)}, u32[]{:S(2)}) collective-permute-start(bf16[32,64,128]{2,1,0:T(8,128)(2,1)} %get-tuple-element.26), channel_id=1, source_target_pairs={{0,1},{1,0},{2,3},{3,2},{4,5},{5,4},{6,7},{7,6},{8,9},{9,8},{10,11... | collective-permute-start | bytes 1572872 | tf_op jit(solution)/shard_map/ppermute | solution.py:582
  139.7 1.0 copy-start.4
  140.7 0.8 copy-start.5
  141.5 15.4 %copy-start = (s32[2]{0:T(128)S(1)}, s32[2]{0:T(128)}, u32[]{:S(2)}) copy-start(s32[2]{0:T(128)} %pad_add_fusion.place_ref) | copy-start | bytes 28
